TPU v7x, 512 devices: a whole 4x4x16 slice. The times are simulated.
512 devices in a mesh: lon: 32 (over z_lo, y), lat: 16 (over x, z_hi, core).
Axes of the slice: x: 4, y: 4, z: 16 (z_hi: 2, z_lo: 8; z = z_hi * 8 + z_lo), core: 2. Of those that a mesh axis runs over, the one named last changes fastest.
Arguments:
- heat_anomaly: float32 [75, 128, 4096], P(None, 'lat', 'lon'), may hold values from -6 to 6
- saltiness_anomaly: float32 [75, 128, 4096], P(None, 'lat', 'lon'), may hold values from -6 to 6
- zonal_edge_current: float32 [75, 128, 4096], P(None, 'lat', 'lon'), may hold values from -3 to 3
- meridional_edge_current: float32 [75, 128, 4096], P(None, 'lat', 'lon'), may hold values from -3 to 3
- interface_mixing_coefficient: float32 [74, 128, 4096], P(None, 'lat', 'lon'), may hold values from 0.05 to 5
- ocean_layer_number: int32 [128, 4096], P('lat', 'lon'), may hold values from 0 to 75, as said below
Outputs:
- heat_next: float32 [75, 128, 4096], P(None, 'lat', 'lon')
- saltiness_next: float32 [75, 128, 4096], P(None, 'lat', 'lon')
- zonal_current_next: float32 [75, 128, 4096], P(None, 'lat', 'lon')
- meridional_current_next: float32 [75, 128, 4096], P(None, 'lat', 'lon')
Inputs may be any that keep to these rules, and one draw needn't show every extreme that they name: `ocean_layer_number`: 0 marks a land column.
All inputs are finite; a program needn't handle non-finite values.
Results may differ from a plain program's by a relative error of at most 0.0003.
Values sent between devices are 32-bit elements; how exact they have to be, the bound alone decides.
No kernel may reach another device: no remote copies, remote signals or barrier semaphores. Data moves between devices by JAX's collectives and lax.ppermute only.
A program may use at most 64 MiB of HBM per device.

v0:
```python
import jax
import jax.numpy as jnp
from jax import lax
from jax.sharding import PartitionSpec as P

time_step = 0.2
diffusion = 0.5
viscosity = 0.5
vertical_viscosity = 0.5
pressure_coef = 0.05
coriolis_coef = 1.5
thermal_coef = 1.0
thermal_curve = 0.2
haline_coef = 0.8
cabbeling_coef = 0.1


def padded_2(block, sides, width, periodic):
    for axis, dim in sides:
        count = lax.axis_size(axis)
        forward = [(i, i + 1) for i in range(count - 1)]
        if periodic:
            forward.append((count - 1, 0))
        backward = [(target, source) for source, target in forward]
        low = lax.ppermute(
            lax.slice_in_dim(block, block.shape[dim] - width, None, axis=dim), axis, forward
        )
        high = lax.ppermute(lax.slice_in_dim(block, 0, width, axis=dim), axis, backward)
        block = jnp.concatenate([low, block, high], axis=dim)
    return block


def tendencies(heat_grid_values, salt_field, eastward, northward, depth_field, coriolis):
    layer_number = heat_grid_values.shape[0]
    heights = jnp.arange(layer_number, dtype=jnp.float32)[:, None, None] + 0.5
    ocean = (heights < depth_field[None]).astype(jnp.float32)
    density = ocean * (
        -thermal_coef * (1.0 + 0.5 * thermal_curve * heat_grid_values) * heat_grid_values
        + haline_coef * salt_field
        - cabbeling_coef * heat_grid_values * salt_field
    )
    pressure = pressure_coef * (jnp.cumsum(density, axis=0) - 0.5 * density)
    east_open = ocean[:, 1:-1, :-1] * ocean[:, 1:-1, 1:]
    north_open = ocean[:, :-1, 1:-1] * ocean[:, 1:, 1:-1]
    ocean_mid = ocean[:, 1:-1, 1:-1]
    stars = []
    for tracer in (heat_grid_values, salt_field):
        flux_east = east_open * (
            eastward[:, 1:-1, :-1] * 0.5 * (tracer[:, 1:-1, :-1] + tracer[:, 1:-1, 1:])
            - diffusion * (tracer[:, 1:-1, 1:] - tracer[:, 1:-1, :-1])
        )
        flux_north = north_open * (
            northward[:, :-1, 1:-1] * 0.5 * (tracer[:, :-1, 1:-1] + tracer[:, 1:, 1:-1])
            - diffusion * (tracer[:, 1:, 1:-1] - tracer[:, :-1, 1:-1])
        )
        change = (
            flux_east[:, :, 1:]
            - flux_east[:, :, :-1]
            + flux_north[:, 1:, :]
            - flux_north[:, :-1, :]
        )
        stars.append(ocean_mid * (tracer[:, 1:-1, 1:-1] - time_step * change))
    east_mid = east_open[:, :, 1:]
    north_mid = north_open[:, 1:, :]
    zonal_mid = eastward[:, 1:-1, 1:-1]
    merid_mid = northward[:, 1:-1, 1:-1]
    north_avg = 0.25 * (
        merid_mid + northward[:, 1:-1, 2:] + northward[:, :-2, 1:-1] + northward[:, :-2, 2:]
    )
    east_avg = 0.25 * (
        zonal_mid + eastward[:, 1:-1, :-2] + eastward[:, 2:, 1:-1] + eastward[:, 2:, :-2]
    )
    zonal_laplacian = (
        eastward[:, 1:-1, 2:]
        + eastward[:, 1:-1, :-2]
        + eastward[:, 2:, 1:-1]
        + eastward[:, :-2, 1:-1]
        - 4.0 * zonal_mid
    )
    merid_laplacian = (
        northward[:, 1:-1, 2:]
        + northward[:, 1:-1, :-2]
        + northward[:, 2:, 1:-1]
        + northward[:, :-2, 1:-1]
        - 4.0 * merid_mid
    )
    press_mid = pressure[:, 1:-1, 1:-1]
    east_star = east_mid * (
        zonal_mid
        + time_step
        * (coriolis * north_avg - (pressure[:, 1:-1, 2:] - press_mid) + viscosity * zonal_laplacian)
    )
    north_star = north_mid * (
        merid_mid
        + time_step
        * (-coriolis * east_avg - (pressure[:, 2:, 1:-1] - press_mid) + viscosity * merid_laplacian)
    )
    return (stars[0], stars[1], east_star, north_star, ocean_mid, east_mid, north_mid)


def banded_thomas_elimination(coupling, source):
    layer_number = source.shape[0]
    upper_prime = []
    source_prime = []
    for level_index in range(layer_number):
        divisor = jnp.ones_like(source[level_index])
        numerator = source[level_index]
        if level_index > 0:
            lower_here = -time_step * coupling[level_index - 1]
            divisor = divisor - lower_here - lower_here * upper_prime[level_index - 1]
            numerator = numerator - lower_here * source_prime[level_index - 1]
        if level_index < layer_number - 1:
            upper_here = -time_step * coupling[level_index]
            divisor = divisor - upper_here
            upper_prime.append(upper_here / divisor)
        else:
            upper_prime.append(jnp.zeros_like(numerator))
        source_prime.append(numerator / divisor)
    solved = [None] * layer_number
    solved[layer_number - 1] = source_prime[layer_number - 1]
    for level_index in range(layer_number - 2, -1, -1):
        solved[level_index] = (
            source_prime[level_index] - upper_prime[level_index] * solved[level_index + 1]
        )
    return jnp.stack(solved, axis=0)


def fold_row(top_row):
    flipped = top_row[:, ::-1]
    lon_count = lax.axis_size("lon")
    field_count = flipped.shape[0]
    row_width = flipped.shape[1]
    piece_width = (row_width + lon_count - 1) // lon_count
    pieces = flipped.reshape(field_count, lon_count, piece_width)
    for turn_index in range(2):
        if turn_index > 0:
            pieces = pieces[:, ::-1, :]
        pieces = lax.all_to_all(pieces, "lon", split_axis=1, concat_axis=1, tiled=True)
    return pieces.reshape(field_count, lon_count * piece_width)


def local(
    heat_anomaly,
    saltiness_anomaly,
    zonal_edge_current,
    meridional_edge_current,
    interface_mixing_coefficient,
    ocean_layer_number,
):
    layer_number = heat_anomaly.shape[0]
    parallel_number = heat_anomaly.shape[1]
    lat_count = lax.axis_size("lat")
    lat_place = lax.axis_index("lat")
    at_top = lat_place == lat_count - 1
    upright_sweeps = ocean_layer_number.astype(jnp.float32)[None]
    stacked_tracers = jnp.concatenate(
        [
            heat_anomaly,
            saltiness_anomaly,
            zonal_edge_current,
            meridional_edge_current,
            upright_sweeps,
        ],
        axis=0,
    )
    field_count = stacked_tracers.shape[0]
    parity = jnp.concatenate(
        [
            jnp.ones((2 * layer_number,), jnp.float32),
            -jnp.ones((2 * layer_number,), jnp.float32),
            jnp.ones((1,), jnp.float32),
        ]
    )[:, None]
    lat_extended = padded_2(stacked_tracers, (("lat", 1),), 1, False)
    mirror = fold_row(stacked_tracers[:, parallel_number - 1, :]) * parity
    ghost_row = jnp.where(at_top, mirror, lat_extended[:, parallel_number + 1, :])
    lat_extended = lat_extended.at[:, parallel_number + 1, :].set(ghost_row)
    extended = padded_2(lat_extended, (("lon", 2),), 1, True)
    ghost_row = extended[:, parallel_number + 1, :]
    shifted = jnp.concatenate([ghost_row[:, 1:], ghost_row[:, -1:]], axis=1)
    field_ids = jnp.arange(field_count)[:, None]
    is_zonal = (field_ids >= 2 * layer_number) & (field_ids < 3 * layer_number)
    fixed_row = jnp.where(jnp.logical_and(at_top, is_zonal), shifted, ghost_row)
    extended = extended.at[:, parallel_number + 1, :].set(fixed_row)
    heat_grid_values = extended[:layer_number]
    salt_field = extended[layer_number : 2 * layer_number]
    eastward = extended[2 * layer_number : 3 * layer_number]
    northward = extended[3 * layer_number : 4 * layer_number]
    depth_field = extended[4 * layer_number]
    row_centres = (lat_place * parallel_number + jnp.arange(parallel_number)).astype(jnp.float32)
    total_rows = parallel_number * lat_count
    coriolis = (coriolis_coef * (2.0 * (row_centres + 0.5) / total_rows - 1.0))[None, :, None]
    heat_interim_guess, salt_star, east_star, north_star, ocean_mid, east_mid, north_mid = (
        tendencies(heat_grid_values, salt_field, eastward, northward, depth_field, coriolis)
    )
    scalar_coupling_coefs = interface_mixing_coefficient * ocean_mid[1:]
    coupling = jnp.stack(
        [
            scalar_coupling_coefs,
            scalar_coupling_coefs,
            vertical_viscosity * east_mid[1:],
            vertical_viscosity * north_mid[1:],
        ],
        axis=1,
    )
    sources = jnp.stack([heat_interim_guess, salt_star, east_star, north_star], axis=1)
    solved = banded_thomas_elimination(coupling, sources)
    return (solved[:, 0], solved[:, 1], solved[:, 2], solved[:, 3])


def solution(mesh):
    placed = (
        P(None, "lat", "lon"),
        P(None, "lat", "lon"),
        P(None, "lat", "lon"),
        P(None, "lat", "lon"),
        P(None, "lat", "lon"),
        P("lat", "lon"),
    )
    return jax.shard_map(
        local,
        mesh=mesh,
        in_specs=placed,
        out_specs=(
            P(None, "lat", "lon"),
            P(None, "lat", "lon"),
            P(None, "lat", "lon"),
            P(None, "lat", "lon"),
        ),
        check_vma=False,
    )
```

profile of v0, /device:TPU:6, one launch (start us, length us, event | category | flops | bytes accessed | tf_op | source)
XLA Modules:
  0.0 141.5 jit_solution(17401426860801001404)
XLA Ops:
  0.7 1.2 copy.905
  1.9 1.2 copy.906
  3.4 1.0 copy.908
  4.4 1.0 copy.909
  5.4 2.0 %concatenate.21 = f32[301,8,128]{0,2,1:T(8,128)S(1)} concatenate(f32[75,8,128]{0,2,1:T(8,128)S(1)} %copy.905, f32[75,8,128]{0,2,1:T(8,128)S(1)} %copy.906, f32[75,8,128]{0,2,1:T(8,128)S(1)} %copy.907, f32[75,8,128]{0,2,1:T(8,128)} %copy.908, f32[1,8,128]{0,2,1:T(8,128)} %copy.909), dimensions={0} | concatenate | bytes 2465792 | tf_op jit(solution)/shard_map/concatenate | solution.py:156
  7.7 32.1 %all_to_all.10 = f32[301,32,4]{0,2,1:T(4,128)S(1)} all-to-all(f32[301,32,4]{0,2,1:T(4,128)S(1)} %reshape.275), channel_id=1, replica_groups=mesh['lon'=32,'lat'=16] {'lon'}, dimensions={1} | all-to-all | bytes 308224 | tf_op jit(solution)/shard_map/all_to_all | solution.py:138
  40.5 5.3 %all-to-all-start.1 = ((f32[301,32,4]{0,2,1:T(4,128)}), f32[301,32,4]{0,2,1:T(4,128)S(1)}, u32[]{:S(2)}, u32[]{:S(2)}) async-start(f32[301,32,4]{0,2,1:T(4,128)} %rev.7), calls=%async_computation.1 | async-start | bytes 393216 | tf_op jit(solution)/shard_map/all_to_all | solution.py:138
  45.8 7.3 %collective-permute-start.1 = (f32[301,1,128]{0,2,1:T(8,128)S(1)}, f32[301,1,128]{0,2,1:T(8,128)S(1)}, u32[]{:S(2)}, u32[]{:S(2)}) collective-permute-start(f32[301,1,128]{0,2,1:T(8,128)S(1)} %get-tuple-element.263), channel_id=1, source_target_pairs={{1,0},{2,1},{3,2},{4,3},{5,4},{6,5},{7,6},{8,7},{9,8},{10,9},{11,1... | collective-permute-start | bytes 462344 | tf_op jit(solution)/shard_map/ppermute | solution.py:28
  53.1 1.9 %collective-permute-start = (f32[301,1,128]{0,2,1:T(8,128)S(1)}, f32[301,1,128]{0,2,1:T(8,128)S(1)}, u32[]{:S(2)}, u32[]{:S(2)}) collective-permute-start(f32[301,1,128]{0,2,1:T(8,128)S(1)} %get-tuple-element.264), channel_id=1, source_target_pairs={{0,1},{1,2},{2,3},{3,4},{4,5},{5,6},{6,7},{7,8},{8,9},{9,10},{10,1... | collective-permute-start | bytes 462344 | tf_op jit(solution)/shard_map/ppermute | solution.py:25
  55.1 1.2 collective-permute-done.1
  56.3 25.4 %collective-permute-done = f32[301,1,128]{0,2,1:T(8,128)S(1)} collective-permute-done((f32[301,1,128]{0,2,1:T(8,128)S(1)}, f32[301,1,128]{0,2,1:T(8,128)S(1)}, u32[]{:S(2)}, u32[]{:S(2)}) %collective-permute-start) | collective-permute-done | bytes 154144 | tf_op jit(solution)/shard_map/ppermute | solution.py:25
  81.7 1.6 %pad_maximum_fusion.1 = f32[301,10,128]{0,2,1:T(8,128)S(1)} fusion(f32[301,1,128]{0,2,1:T(8,128)S(1)} %collective-permute-done.1, f32[301,8,128]{0,2,1:T(8,128)} %copy-done.2, f32[301,1,128]{0,2,1:T(8,128)S(1)} %collective-permute-done), kind=kLoop, calls=%fused_computation.1 | loop fusion | flops 770560 | bytes 3082240 | tf_op jit(solution)/shard_map/concatenate | solution.py:29
  83.4 7.9 %collective-permute-start.3 = (f32[301,10,1]{0,2,1:T(1,128)S(1)}, f32[301,10,1]{0,2,1:T(1,128)S(1)}, u32[]{:S(2)}, u32[]{:S(2)}) collective-permute-start(f32[301,10,1]{0,2,1:T(1,128)S(1)} %get-tuple-element.261), channel_id=1, source_target_pairs={{16,0},{32,16},{48,32},{64,48},{80,64},{96,80},{112,96},{128,112},... | collective-permute-start | bytes 36128 | tf_op jit(solution)/shard_map/ppermute | solution.py:28
  91.3 1.9 %collective-permute-start.2 = (f32[301,10,1]{0,2,1:T(1,128)S(1)}, f32[301,10,1]{0,2,1:T(1,128)S(1)}, u32[]{:S(2)}, u32[]{:S(2)}) collective-permute-start(f32[301,10,1]{0,2,1:T(1,128)S(1)} %get-tuple-element.260), channel_id=1, source_target_pairs={{0,16},{16,32},{32,48},{48,64},{64,80},{80,96},{96,112},{112,128},... | collective-permute-start | bytes 36128 | tf_op jit(solution)/shard_map/ppermute | solution.py:25
  93.3 12.4 %collective-permute-done.2 = f32[301,10,1]{0,2,1:T(1,128)S(1)} collective-permute-done((f32[301,10,1]{0,2,1:T(1,128)S(1)}, f32[301,10,1]{0,2,1:T(1,128)S(1)}, u32[]{:S(2)}, u32[]{:S(2)}) %collective-permute-start.2) | collective-permute-done | bytes 12072 | tf_op jit(solution)/shard_map/ppermute | solution.py:25
  105.7 1.7 %pad_maximum_fusion = f32[301,10,130]{0,2,1:T(8,128)S(1)} fusion(f32[301,10,1]{0,2,1:T(1,128)S(1)} %collective-permute-done.3, f32[301,10,128]{0,2,1:T(8,128)} %copy-done.1, f32[301,10,1]{0,2,1:T(1,128)S(1)} %collective-permute-done.2), kind=kLoop, calls=%fused_computation | loop fusion | flops 782600 | bytes 3130400 | tf_op jit(solution)/shard_map/concatenate | solution.py:29
  107.4 5.5 %copy.914 = f32[301,10,130]{2,1,0:T(8,128)} copy(f32[301,10,130]{0,2,1:T(8,128)S(1)} %pad_maximum_fusion) | data formatting | bytes 3130400 | tf_op jit(solution)/shard_map/concatenate | solution.py:29
  112.9 2.0 %slice.994 = f32[301,1,130]{2,1,0:T(1,128)S(1)} slice(f32[301,10,130]{2,1,0:T(8,128)} %copy.914), slice={[0:301], [9:10], [0:130]} | slice | bytes 313040 | tf_op jit(solution)/shard_map/slice | solution.py:179
  115.4 2.8 %broadcast_select_fusion = f32[301,1,130]{2,1,0:T(1,128)S(1)} fusion(pred[301]{0:T(512)(128)(4,1)S(1)} %fusion.384, f32[301,1,1]{2,1,0:T(1,128)S(1)} %copy.913, f32[301,1,129]{2,1,0:T(1,128)S(1)} %copy.912, f32[301,10,130]{2,1,0:T(8,128)} %copy.914), kind=kLoop, calls=%fused_computation.7 | loop fusion | flops 78260 | bytes 469861 | tf_op jit(solution)/shard_map/jit(_where)/select_n | solution.py:183
  118.2 8.2 %scatter.9 = f32[301,10,130]{2,1,0:T(8,128)} dynamic-update-slice(f32[301,10,130]{2,1,0:T(8,128)} %copy.914, f32[301,1,130]{2,1,0:T(1,128)S(1)} %broadcast_select_fusion, s32[]{:T(128)} %constant.90.clone.1, s32[]{:T(128)} %constant.91.clone.1, s32[]{:T(128)} %constant.90.clone.1) | dynamic-update-slice | bytes 313044 | tf_op jit(solution)/shard_map/scatter | solution.py:184
  127.2 3.9 %subtract_multiply_fusion = f32[75,10,130]{2,1,0:T(8,128)S(1)} fusion(f32[301,10,130]{2,1,0:T(8,128)} %scatter.9, f32[10,130]{1,0:T(8,128)S(1)} %slice_bitcast_fusion.5, f32[75]{0:T(128)S(1)} %iota_add_fusion), kind=kOutput, calls=%fused_computation.5 | output fusion | flops 9457500 | bytes 5338992 | tf_op jit(solution)/shard_map/jit(cumsum)/reduce_window_sum | solution.py:42
  131.4 0.9 subtract_multiply_fusion.3
  134.6 0.9 fusion.16
  140.5 1.0 slice_bitcast_fusion
  (125 shorter events, 9.4 us)
Async XLA Ops:
  0.6 2.5 %copy-start.3 = (f32[75,8,128]{2,1,0:T(8,128)S(1)}, f32[75,8,128]{2,1,0:T(8,128)}, u32[]{:S(2)}) copy-start(f32[75,8,128]{2,1,0:T(8,128)} %param.12) | copy-start | bytes 921604
  0.6 2.7 %copy-start.4 = (f32[75,8,128]{2,1,0:T(8,128)S(1)}, f32[75,8,128]{2,1,0:T(8,128)}, u32[]{:S(2)}) copy-start(f32[75,8,128]{2,1,0:T(8,128)} %param.13) | copy-start | bytes 921604
  1.9 2.5 %copy-start.6 = (s32[8,128]{1,0:T(8,128)S(1)}, s32[8,128]{1,0:T(8,128)}, u32[]{:S(2)}) copy-start(s32[8,128]{1,0:T(8,128)} %param.15) | copy-start | bytes 12292
  7.5 33.0 %copy-start.2 = (f32[301,8,128]{0,2,1:T(8,128)}, f32[301,8,128]{0,2,1:T(8,128)S(1)}, u32[]{:S(2)}) copy-start(f32[301,8,128]{0,2,1:T(8,128)S(1)} %concatenate.21) | copy-start | bytes 3698692
  40.5 42.7 %all-to-all-start.1 = ((f32[301,32,4]{0,2,1:T(4,128)}), f32[301,32,4]{0,2,1:T(4,128)S(1)}, u32[]{:S(2)}, u32[]{:S(2)}) async-start(f32[301,32,4]{0,2,1:T(4,128)} %rev.7), calls=%async_computation.1 | async-start | bytes 393216 | tf_op jit(solution)/shard_map/all_to_all | solution.py:138
  45.8 10.5 %collective-permute-start.1 = (f32[301,1,128]{0,2,1:T(8,128)S(1)}, f32[301,1,128]{0,2,1:T(8,128)S(1)}, u32[]{:S(2)}, u32[]{:S(2)}) collective-permute-start(f32[301,1,128]{0,2,1:T(8,128)S(1)} %get-tuple-element.263), channel_id=1, source_target_pairs={{1,0},{2,1},{3,2},{4,3},{5,4},{6,5},{7,6},{8,7},{9,8},{10,9},{11,1... | collective-permute-start | bytes 462344 | tf_op jit(solution)/shard_map/ppermute | solution.py:28
  53.1 28.6 %collective-permute-start = (f32[301,1,128]{0,2,1:T(8,128)S(1)}, f32[301,1,128]{0,2,1:T(8,128)S(1)}, u32[]{:S(2)}, u32[]{:S(2)}) collective-permute-start(f32[301,1,128]{0,2,1:T(8,128)S(1)} %get-tuple-element.264), channel_id=1, source_target_pairs={{0,1},{1,2},{2,3},{3,4},{4,5},{5,6},{6,7},{7,8},{8,9},{9,10},{10,1... | collective-permute-start | bytes 462344 | tf_op jit(solution)/shard_map/ppermute | solution.py:25
  55.1 28.3 %copy-start.7 = (f32[301]{0:T(512)S(1)}, f32[301]{0:T(512)}, u32[]{:S(2)}) copy-start(f32[301]{0:T(512)} %constant.89.clone.1) | copy-start | bytes 3616
  83.4 9.9 %copy-start.1 = (f32[301,10,128]{0,2,1:T(8,128)}, f32[301,10,128]{0,2,1:T(8,128)S(1)}, u32[]{:S(2)}) copy-start(f32[301,10,128]{0,2,1:T(8,128)S(1)} %select_dynamic-update-slice_fusion) | copy-start | bytes 4623364
  83.4 9.9 %collective-permute-start.3 = (f32[301,10,1]{0,2,1:T(1,128)S(1)}, f32[301,10,1]{0,2,1:T(1,128)S(1)}, u32[]{:S(2)}, u32[]{:S(2)}) collective-permute-start(f32[301,10,1]{0,2,1:T(1,128)S(1)} %get-tuple-element.261), channel_id=1, source_target_pairs={{16,0},{32,16},{48,32},{64,48},{80,64},{96,80},{112,96},{128,112},... | collective-permute-start | bytes 36128 | tf_op jit(solution)/shard_map/ppermute | solution.py:28
  91.3 14.3 %collective-permute-start.2 = (f32[301,10,1]{0,2,1:T(1,128)S(1)}, f32[301,10,1]{0,2,1:T(1,128)S(1)}, u32[]{:S(2)}, u32[]{:S(2)}) collective-permute-start(f32[301,10,1]{0,2,1:T(1,128)S(1)} %get-tuple-element.260), channel_id=1, source_target_pairs={{0,16},{16,32},{32,48},{48,64},{64,80},{80,96},{96,112},{112,128},... | collective-permute-start | bytes 36128 | tf_op jit(solution)/shard_map/ppermute | solution.py:25
  127.2 4.2 %copy-start = (f32[301,10,130]{2,1,0:T(8,128)S(1)}, f32[301,10,130]{2,1,0:T(8,128)}, u32[]{:S(2)}) copy-start(f32[301,10,130]{2,1,0:T(8,128)} %scatter.9) | copy-start | bytes 4695604
  134.6 1.0 copy-start.5
where the time goes:
time: 142 us
  waiting for transfers between devices  39 us (27%)
  blocking collectives  32.1 us (23%)
  local copies, waits for them, and re-layouts  26.1 us (18%)
  starting transfers between devices  24.3 us (17%)
  other arithmetic  18.5 us (13%)
  between operations  1.56 us (1%)
    ppermute x2, waiting for transfers between devices, padded_2(): lax.ppermute(lax.slice_in_dim(block, block.shape[dim] - width, None, axis...  37.8 us
    all_to_all x1, blocking collectives, fold_row(): lax.all_to_all(pieces, 'lon', split_axis=1, concat_axis=1, tiled=True)  32.1 us
    ppermute x2, starting transfers between devices, padded_2(): lax.ppermute(lax.slice_in_dim(block, 0, width, axis=dim), axis, backward)  15.2 us
    scatter x1, local copies, waits for them, and re-layouts, local(): extended = extended.at[:, parallel_number + 1, :].set(fixed_row)  8.24 us
    concatenate x1, local copies, waits for them, and re-layouts, padded_2(): block = jnp.concatenate([low, block, high], axis=dim)  5.52 us
    all_to_all x1, starting transfers between devices, fold_row(): lax.all_to_all(pieces, 'lon', split_axis=1, concat_axis=1, tiled=True)  5.25 us
    unnamed x57, local copies, waits for them, and re-layouts  4 us
    another operation x1, other arithmetic, tendencies(): pressure = pressure_coef * (jnp.cumsum(density, axis=0) - 0.5 * density)  3.95 us
  transfers between devices with their start and end apart: 5, of which 3 were waited for; matrix products, arithmetic and copies ran while one was open for 1% of the time, Pallas kernels for 0%

commit v1 on v0

v1 whole, which is shorter than its diff:
```python
import jax
import jax.numpy as jnp
from jax import lax
from jax.experimental import pallas as pl
from jax.experimental.pallas import tpu as pltpu
from jax.sharding import PartitionSpec as P

DT = 0.2
CORIOLIS = 1.5
PRESSURE = 0.05
VISC_STEP = 0.1

ROWS, LANES = 8, 128
COL_ROWS = 40


def elimination_constants(levels):
    inner, last = [], []
    for k in range(levels):
        above = VISC_STEP * VISC_STEP * inner[k - 1] if k else 0.0
        step = VISC_STEP if k else 0.0
        inner.append(1.0 / (1.0 + step + VISC_STEP - above))
        last.append(1.0 / (1.0 + step - above))
    return inner, last


def lane_ids():
    return lax.broadcasted_iota(jnp.int32, (ROWS, LANES), 1)


def row_ids():
    return lax.broadcasted_iota(jnp.int32, (ROWS, LANES), 0)


def roll(x, shift, axis):
    return pltpu.roll(x, shift % x.shape[axis], axis)


def density_of(t, s):
    return -(1.0 + 0.1 * t) * t + 0.8 * s - 0.1 * t * s


def level_to_lane(rows, lane):
    k = lax.broadcasted_iota(jnp.int32, rows.shape, 0)
    l = lax.broadcasted_iota(jnp.int32, rows.shape, 1)
    return jnp.sum(jnp.where(k == l, rows[:, lane : lane + 1], 0.0), axis=0, keepdims=True)


def pack_rows(place, levels, t, s, u, v, depth, to_a, to_b, corner):
    even = lax.rem(place[0], 2) == 0
    packed = []
    for f, ref in enumerate((t, s, u, v)):
        top = ref[pl.ds(ROWS - 1, levels, stride=ROWS), :]
        low = ref[pl.ds(0, levels, stride=ROWS), :]
        to_a[pl.ds(f, levels, stride=4), :] = jnp.where(even, top, low)
        b = jnp.where(even, low, top)
        to_b[pl.ds(f, levels, stride=4), :] = b
        packed.append(b)
    h = depth[...].astype(jnp.float32)
    blank = jnp.zeros((3, LANES), jnp.float32)
    last = 4 * levels
    to_a[last : last + 4, :] = jnp.concatenate([jnp.where(even, h[7:8], h[0:1]), blank], axis=0)
    to_b[last : last + 4, :] = jnp.concatenate([jnp.where(even, h[0:1], h[7:8]), blank], axis=0)
    cu = level_to_lane(packed[2], LANES - 1)
    cv = level_to_lane(packed[3], 0)
    row = row_ids()
    corner[...] = jnp.where(row == 0, cu, jnp.where(row == 1, cv, 0.0))


def pack_columns(place, levels, t, s, u, v, depth, from_a, to_c, to_d):
    lat_even = lax.rem(place[0], 2) == 0
    lon_even = lax.rem(place[1], 2) == 0
    lane = lane_ids()
    h = depth[...].astype(jnp.float32)
    for f, ref in enumerate((t, s, u, v)):
        east = jnp.zeros((ROWS, LANES), jnp.float32)
        west = jnp.zeros((ROWS, LANES), jnp.float32)
        for k in range(levels):
            x = ref[k * ROWS : (k + 1) * ROWS, :]
            east = jnp.where(lane == k, x[:, LANES - 1 : LANES], east)
            west = jnp.where(lane == k, x[:, 0:1], west)
        if f == 0:
            east = jnp.where(lane == levels, h[:, LANES - 1 : LANES], east)
            west = jnp.where(lane == levels, h[:, 0:1], west)
        to_c[f * ROWS : (f + 1) * ROWS, :] = jnp.where(lon_even, east, west)
        to_d[f * ROWS : (f + 1) * ROWS, :] = jnp.where(lon_even, west, east)
    cu = level_to_lane(from_a[pl.ds(2, levels, stride=4), :], LANES - 1)
    cv = level_to_lane(from_a[pl.ds(3, levels, stride=4), :], 0)
    east = jnp.broadcast_to(jnp.where(lat_even, cu, 0.0), (ROWS, LANES))
    west = jnp.broadcast_to(jnp.where(lat_even, 0.0, cv), (ROWS, LANES))
    to_c[4 * ROWS : 5 * ROWS, :] = jnp.where(lon_even, east, west)
    to_d[4 * ROWS : 5 * ROWS, :] = jnp.where(lon_even, west, east)


def coriolis_rows(place, total):
    row = (place[0] * ROWS + row_ids()).astype(jnp.float32)
    return CORIOLIS * (2.0 * (row + 0.5) / total - 1.0)


def local_work(place, levels, total, t, s, u, v, mix, depth, st, ss, su, sv, ra, aa, ba):
    lane, row = lane_ids(), row_ids()
    h = depth[...].astype(jnp.float32)
    f4 = (0.25 * DT) * coriolis_rows(place, total)
    not_e, not_w = lane < LANES - 1, lane > 0
    not_n, not_s = row < ROWS - 1, row > 0
    open_e = jnp.where(not_e, jnp.minimum(h, roll(h, -1, 1)), 0.0)
    open_n = jnp.where(not_n, jnp.minimum(h, roll(h, -1, 0)), 0.0)
    summed = jnp.zeros((ROWS, LANES), jnp.float32)
    b_prev = jnp.zeros((ROWS, LANES), jnp.float32)
    c_here = jnp.zeros((ROWS, LANES), jnp.float32)
    zero = jnp.zeros((ROWS, LANES), jnp.float32)
    for k in range(levels):
        tk, sk, uk, vk = t[k], s[k], u[k], v[k]
        wet = h > float(k)
        dens = jnp.where(wet, density_of(tk, sk), 0.0)
        summed = summed + dens
        p = PRESSURE * (summed - 0.5 * dens)
        me, mn = open_e > float(k), open_n > float(k)
        half_u, half_v = 0.5 * uk, 0.5 * vk
        for x, out in ((tk, st), (sk, ss)):
            xe, xn = roll(x, -1, 1), roll(x, -1, 0)
            fe = jnp.where(me, half_u * (x + xe) - 0.5 * (xe - x), 0.0)
            fn = jnp.where(mn, half_v * (x + xn) - 0.5 * (xn - x), 0.0)
            out[k] = x - DT * (fe - roll(fe, 1, 1) + fn - roll(fn, 1, 0))
        ue = jnp.where(not_e, roll(uk, -1, 1), 0.0)
        uw = jnp.where(not_w, roll(uk, 1, 1), 0.0)
        un = jnp.where(not_n, roll(uk, -1, 0), 0.0)
        us = jnp.where(not_s, roll(uk, 1, 0), 0.0)
        unw = jnp.where(not_n, roll(uw, -1, 0), 0.0)
        ve = jnp.where(not_e, roll(vk, -1, 1), 0.0)
        vw = jnp.where(not_w, roll(vk, 1, 1), 0.0)
        vn = jnp.where(not_n, roll(vk, -1, 0), 0.0)
        vs = jnp.where(not_s, roll(vk, 1, 0), 0.0)
        vse = jnp.where(not_s, roll(ve, 1, 0), 0.0)
        pe = jnp.where(not_e, roll(p, -1, 1), 0.0)
        pn = jnp.where(not_n, roll(p, -1, 0), 0.0)
        su[k] = (
            uk + f4 * (vk + ve + vs + vse) - DT * (pe - p) + 0.1 * (ue + uw + un + us - 4.0 * uk)
        )
        sv[k] = (
            vk - f4 * (uk + uw + un + unw) - DT * (pn - p) + 0.1 * (ve + vw + vn + vs - 4.0 * vk)
        )
        c_next = jnp.where(h > float(k + 1), DT * mix[k], 0.0) if k < levels - 1 else zero
        r = 1.0 / (1.0 + c_here + c_next - c_here * b_prev)
        r = jnp.where(wet, r, 0.0)
        ra[k] = r
        aa[k] = c_here * r
        b_prev = c_next * r
        ba[k] = b_prev
        c_here = c_next


def finish(
    place, levels, total, st, ss, su, sv, ra, aa, ba, depth,
    to_a, to_b, from_a, from_b, to_c, to_d, from_c, from_d, corner,
    ot, os, ou, ov, north, south, east, west, kept,
):
    lane, row = lane_ids(), row_ids()
    lat_even = lax.rem(place[0], 2) == 0
    lon_even = lax.rem(place[1], 2) == 0
    top = place[2] == 1
    h = depth[...].astype(jnp.float32)
    f4 = (0.25 * DT) * coriolis_rows(place, total)
    f7, f0 = f4[7:8, :], f4[0:1, :]

    kk = lax.broadcasted_iota(jnp.int32, (levels, LANES), 0).astype(jnp.float32)
    ll = lax.broadcasted_iota(jnp.int32, (levels, LANES), 1)

    def north_of(f):
        return jnp.where(
            lat_even, from_a[pl.ds(f, levels, stride=4), :], from_b[pl.ds(f, levels, stride=4), :]
        )

    def south_of(f):
        return jnp.where(
            lat_even, from_b[pl.ds(f, levels, stride=4), :], from_a[pl.ds(f, levels, stride=4), :]
        )

    def row_7(f):
        return jnp.where(
            lat_even, to_a[pl.ds(f, levels, stride=4), :], to_b[pl.ds(f, levels, stride=4), :]
        )

    def row_0(f):
        return jnp.where(
            lat_even, to_b[pl.ds(f, levels, stride=4), :], to_a[pl.ds(f, levels, stride=4), :]
        )

    def mirrored(x, last):
        ids = lax.rem(last + LANES - lax.broadcasted_iota(jnp.int32, x.shape, 1), LANES)
        return jnp.take_along_axis(x, ids, axis=1)

    at = 4 * levels
    h_a, h_b = from_a[at : at + 1, :], from_b[at : at + 1, :]
    h_n = jnp.where(lat_even, h_a, h_b)
    h_s = jnp.where(lat_even, h_b, h_a)
    h_n8 = jnp.broadcast_to(h_n, (ROWS, LANES))
    h_n8 = jnp.where(top, mirrored(h_n8, LANES - 1), h_n8)
    h_n = h_n8[0:1, :]
    tn, sn, un, vn = (north_of(f) for f in range(4))
    tn = jnp.where(top, mirrored(tn, LANES - 1), tn)
    sn = jnp.where(top, mirrored(sn, LANES - 1), sn)
    vn = jnp.where(top, -mirrored(vn, LANES - 1), vn)
    un = jnp.where(top, -mirrored(un, LANES - 2), un)
    unw = roll(un, 1, 1)
    unw = jnp.where(jnp.logical_or(top, ll > 0), unw, 0.0)
    un = jnp.where(jnp.logical_and(top, ll == LANES - 1), 0.0, un)
    t7, s7, v7 = row_7(0), row_7(1), row_7(3)
    mask = jnp.minimum(h[7:8, :], h_n) > kk
    north[0, :levels, :] = jnp.where(mask, -0.1 * (v7 * (t7 + tn) - (tn - t7)), 0.0)
    north[1, :levels, :] = jnp.where(mask, -0.1 * (v7 * (s7 + sn) - (sn - s7)), 0.0)
    north[2, :levels, :] = 0.1 * un
    north[3, :levels, :] = 0.1 * vn - f7 * (un + unw)
    north[4, :levels, :] = jnp.where(h_n > kk, (DT * PRESSURE) * density_of(tn, sn), 0.0)

    ts, ssouth, us, vs = (south_of(f) for f in range(4))
    t0, s0 = row_0(0), row_0(1)
    mask = jnp.minimum(h[0:1, :], h_s) > kk
    south[0, :levels, :] = jnp.where(mask, 0.1 * (vs * (ts + t0) - (t0 - ts)), 0.0)
    south[1, :levels, :] = jnp.where(mask, 0.1 * (vs * (ssouth + s0) - (s0 - ssouth)), 0.0)
    vse = jnp.where(ll < LANES - 1, roll(vs, -1, 1), 0.0)
    south[2, :levels, :] = 0.1 * us + f0 * (vs + vse)
    south[3, :levels, :] = 0.1 * vs

    def tile(even_ref, odd_ref, f):
        at = slice(f * ROWS, (f + 1) * ROWS)
        return jnp.where(lon_even, even_ref[at, :], odd_ref[at, :])

    kl = lane.astype(jnp.float32)
    te, se, ue, ve, ce = (tile(from_c, from_d, f) for f in range(5))
    tw, sw, uw, vw, cw = (tile(from_d, from_c, f) for f in range(5))
    t127, s127, u127 = (tile(to_c, to_d, f) for f in range(3))
    tz, sz = (tile(to_d, to_c, f) for f in range(2))
    cb_u = jnp.broadcast_to(corner[0:1, :], (ROWS, LANES))
    cb_v = jnp.broadcast_to(corner[1:2, :], (ROWS, LANES))
    south_east = jnp.where(lat_even, cb_v, ce)
    north_west = jnp.where(lat_even, cw, jnp.where(top, 0.0, cb_u))
    north_end = jnp.where(top, -cb_u, 0.0)
    h_e = te[:, levels : levels + 1]
    h_w = tw[:, levels : levels + 1]
    mask = jnp.minimum(h[:, LANES - 1 : LANES], h_e) > kl
    dt_e = jnp.where(mask, -0.1 * (u127 * (t127 + te) - (te - t127)), 0.0)
    ds_e = jnp.where(mask, -0.1 * (u127 * (s127 + se) - (se - s127)), 0.0)
    mask = jnp.minimum(h[:, 0:1], h_w) > kl
    dt_w = jnp.where(mask, 0.1 * (uw * (tw + tz) - (tz - tw)), 0.0)
    ds_w = jnp.where(mask, 0.1 * (uw * (sw + sz) - (sz - sw)), 0.0)
    dens = jnp.where(h_e > kl, density_of(te, se), 0.0)
    summed = dens
    for step in (1, 2, 4, 8, 16, 32, 64):
        summed = summed + jnp.where(lane >= step, roll(summed, step, 1), 0.0)
    pe = PRESSURE * (summed - 0.5 * dens)
    ve_up = jnp.where(row > 0, roll(ve, 1, 0), south_east)
    uw_dn = jnp.where(row < ROWS - 1, roll(uw, -1, 0), north_west)
    end = jnp.where(row == ROWS - 1, north_end, 0.0)
    du_e = f4 * (ve + ve_up) - DT * pe + 0.1 * ue + 0.1 * end
    du_w = 0.1 * uw
    dv_e = 0.1 * ve - f4 * end
    dv_w = 0.1 * vw - f4 * (uw + uw_dn)

    m_u = jnp.minimum(h, jnp.where(lane < LANES - 1, roll(h, -1, 1), h_e))
    m_v = jnp.minimum(h, jnp.where(row < ROWS - 1, roll(h, -1, 0), h_n))
    at_n, at_s = row == ROWS - 1, row == 0
    at_e, at_w = lane == LANES - 1, lane == 0
    inner, last = elimination_constants(levels)
    pt = ps = pu = pv = jnp.zeros((ROWS, LANES), jnp.float32)
    cs = jnp.zeros((1, LANES), jnp.float32)
    for k in range(levels):
        def spread(f, de, dw, extra=None):
            n = north[f, k : k + 1, :]
            if extra is not None:
                n = n - extra
            base = jnp.where(at_n, n, jnp.where(at_s, south[f, k : k + 1, :], 0.0))
            side = jnp.where(at_e, de[:, k : k + 1], jnp.where(at_w, dw[:, k : k + 1], 0.0))
            return base + side

        dn = north[4, k : k + 1, :]
        cs = cs + dn
        r, a = ra[k], aa[k]
        pt = r * (st[k] + spread(0, dt_e, dt_w)) + a * pt
        ps = r * (ss[k] + spread(1, ds_e, ds_w)) + a * ps
        ru = jnp.where(m_u > float(k + 1), inner[k], jnp.where(m_u > float(k), last[k], 0.0))
        rv = jnp.where(m_v > float(k + 1), inner[k], jnp.where(m_v > float(k), last[k], 0.0))
        pu = ru * (su[k] + spread(2, du_e, du_w)) + (VISC_STEP * ru) * pu
        pv = rv * (sv[k] + spread(3, dv_e, dv_w, cs - 0.5 * dn)) + (VISC_STEP * rv) * pv
        kept[0, k] = pt
        kept[1, k] = ps
        kept[2, k] = pu
        kept[3, k] = pv
    xt, xs, xu, xv = pt, ps, pu, pv
    for k in range(levels - 1, -1, -1):
        if k < levels - 1:
            b = ba[k]
            bu = jnp.where(m_u > float(k + 1), VISC_STEP * inner[k], 0.0)
            bv = jnp.where(m_v > float(k + 1), VISC_STEP * inner[k], 0.0)
            xt = kept[0, k] + b * xt
            xs = kept[1, k] + b * xs
            xu = kept[2, k] + bu * xu
            xv = kept[3, k] + bv * xv
        ot[k] = xt
        os[k] = xs
        ou[k] = xu
        ov[k] = xv


SMEM = pl.BlockSpec(memory_space=pltpu.SMEM)
VMEM = pl.BlockSpec(memory_space=pltpu.VMEM)


def call(body, outs, n_in, scratch=(), name=None):
    return pl.pallas_call(
        body,
        out_shape=tuple(jax.ShapeDtypeStruct(s, jnp.float32) for s in outs),
        in_specs=[SMEM] + [VMEM] * n_in,
        out_specs=tuple(VMEM for _ in outs),
        scratch_shapes=list(scratch),
        name=name,
    )


def exchanges(n_lat, n_lon):
    def at(lat, lon):
        return (lon % n_lon) * n_lat + lat

    def both(x, y):
        return [(x, y), (y, x)]

    a, b, corner, c, d = [], [], [], [], []
    for lon in range(n_lon):
        for lat in range(0, n_lat, 2):
            a += both(at(lat, lon), at(lat + 1, lon))
        for lat in range(1, n_lat - 1, 2):
            b += both(at(lat, lon), at(lat + 1, lon))
            corner += both(at(lat, lon), at(lat + 1, lon - 1))
        b.append((at(n_lat - 1, lon), at(n_lat - 1, n_lon - 1 - lon)))
        corner.append((at(n_lat - 1, lon), at(n_lat - 1, n_lon - 2 - lon)))
    for lat in range(n_lat):
        for lon in range(0, n_lon, 2):
            c += both(at(lat, lon), at(lat, lon + 1))
            d += both(at(lat, lon + 1), at(lat, lon + 2))
    return a, b, corner, c, d


def local(t, s, u, v, mix, depth):
    levels = t.shape[0]
    n_lat, n_lon = lax.axis_size("lat"), lax.axis_size("lon")
    total = float(n_lat * ROWS)
    lat, lon = lax.axis_index("lat"), lax.axis_index("lon")
    place = jnp.stack([lat, lon, (lat == n_lat - 1).astype(jnp.int32)]).astype(jnp.int32)
    pairs_a, pairs_b, pairs_corner, pairs_c, pairs_d = exchanges(n_lat, n_lon)
    axes = ("lon", "lat")
    flat = [x.reshape(levels * ROWS, LANES) for x in (t, s, u, v)]
    row_shape = (4 * levels + 4, LANES)
    full = (levels, ROWS, LANES)

    to_a, to_b, to_corner = call(
        lambda place, *refs: pack_rows(place, levels, *refs),
        [row_shape, row_shape, (ROWS, LANES)], 5, name="pack_rows",
    )(place, *flat, depth)
    from_b = lax.ppermute(to_b, axes, pairs_b)
    corner = lax.ppermute(to_corner, axes, pairs_corner)
    from_a = lax.ppermute(to_a, axes, pairs_a)
    to_c, to_d = call(
        lambda place, *refs: pack_columns(place, levels, *refs),
        [(COL_ROWS, LANES)] * 2, 6, name="pack_columns",
    )(place, *flat, depth, from_a)
    from_d = lax.ppermute(to_d, axes, pairs_d)
    from_c = lax.ppermute(to_c, axes, pairs_c)
    work = call(
        lambda place, *refs: local_work(place, levels, total, *refs), [full] * 7, 6, name="local_work"
    )(place, t, s, u, v, mix, depth)
    padded = (levels + 7) // 8 * 8
    return call(
        lambda place, *refs: finish(place, levels, total, *refs),
        [full] * 4,
        17,
        [
            pltpu.VMEM((5, padded, LANES), jnp.float32),
            pltpu.VMEM((4, padded, LANES), jnp.float32),
            pltpu.VMEM((4, ROWS, LANES), jnp.float32),
            pltpu.VMEM((4, ROWS, LANES), jnp.float32),
            pltpu.VMEM((4,) + full, jnp.float32),
        ],
        name="finish",
    )(place, *work, depth, to_a, to_b, from_a, from_b, to_c, to_d, from_c, from_d, corner)


def solution(mesh):
    field = P(None, "lat", "lon")
    return jax.shard_map(
        local,
        mesh=mesh,
        in_specs=(field,) * 5 + (P("lat", "lon"),),
        out_specs=(field,) * 4,
        check_vma=False,
    )
```

time: 142 us -> 56.1 us (0.40)
  waiting for transfers between devices: 39 us -> 5.87 us
  blocking collectives: 32.1 us -> 0 us
  local copies, waits for them, and re-layouts: 26.1 us -> 1.31 us
  other arithmetic: 18.5 us -> 0.56 us
  Pallas kernels: 0 us -> 16.5 us
  starting transfers between devices: 24.3 us -> 30.8 us
    ppermute x4 -> x5, waiting for transfers between devices: 39 us -> 5.87 us  [the longest x1 5.86 us: local(): corner = lax.ppermute(to_corner, axes, pairs_corner)]
    all_to_all x1 -> x0, blocking collectives: 32.1 us -> none  [fold_row(): lax.all_to_all(pieces, 'lon', split_axis=1, concat_axis=1, tiled=True)]
    pallas_call x0 -> x4, Pallas kernels: none -> 16.5 us  [the longest x1 7.65 us: local(): call(lambda place, *refs: local_work(place, levels, total, *refs), [full]...]
    ppermute x4 -> x5, starting transfers between devices: 19.1 us -> 30.8 us  [the longest x1 16.1 us: local(): from_b = lax.ppermute(to_b, axes, pairs_b)]
    scatter x1 -> x0, local copies, waits for them, and re-layouts: 8.24 us -> none  [local(): extended = extended.at[:, parallel_number + 1, :].set(fixed_row)]
    concatenate x6 -> x0, local copies, waits for them, and re-layouts: 7.92 us -> none  [the longest x1 5.52 us: padded_2(): block = jnp.concatenate([low, block, high], axis=dim)]
    another operation x9 -> x1, other arithmetic: 6.65 us -> 0.56 us  [local(): jnp.stack([lat, lon, (lat == n_lat - 1).astype(jnp.int32)])]
    all_to_all x1 -> x0, starting transfers between devices: 5.25 us -> none  [fold_row(): lax.all_to_all(pieces, 'lon', split_axis=1, concat_axis=1, tiled=True)]
  transfers between devices with their start and end apart: 5 -> 5, of which waited for: 3 -> 1; matrix products, arithmetic and copies ran while one was open for 1% -> 0% of each run, Pallas kernels for 0% -> 19%
where the time goes in v1:
time: 56.1 us; the launch traced here: 55.7 us
  starting transfers between devices  30.8 us (55%)
  Pallas kernels  16.5 us (29%)
  waiting for transfers between devices  5.87 us (10%)
  local copies, waits for them, and re-layouts  1.31 us (2%)
  between operations  0.73 us (1%)
    ppermute x1, starting transfers between devices, local(): from_b = lax.ppermute(to_b, axes, pairs_b)  16.1 us
    pallas_call x1, Pallas kernels, local(): call(lambda place, *refs: local_work(place, levels, total, *refs), [full]...  7.65 us
    ppermute x1, starting transfers between devices, local(): from_d = lax.ppermute(to_d, axes, pairs_d)  7.27 us
    ppermute x1, waiting for transfers between devices, local(): corner = lax.ppermute(to_corner, axes, pairs_corner)  5.86 us
    pallas_call x1, Pallas kernels, local(): call(lambda place, *refs: finish(place, levels, total, *refs), [full] * 4...  4.12 us
    ppermute x1, starting transfers between devices, local(): from_c = lax.ppermute(to_c, axes, pairs_c)  3.6 us
    pallas_call x1, Pallas kernels, local(): call(lambda place, *refs: pack_columns(place, levels, *refs), [(COL_ROWS,...  2.65 us
    pallas_call x1, Pallas kernels, local(): call(lambda place, *refs: pack_rows(place, levels, *refs), [row_shape, ro...  2.04 us
  transfers between devices with their start and end apart: 5, of which 1 were waited for; matrix products, arithmetic and copies ran while one was open for 0% of the time, Pallas kernels for 19%

profile of v1, /device:TPU:6, one launch (start us, length us, event | category | flops | bytes accessed | tf_op | source)
XLA Modules:
  0.0 55.7 jit_solution(5504990907981671548)
XLA Ops:
  0.6 0.6 %pad_add_fusion.place = s32[3]{0:T(128)} fusion(s32[1]{0:T(128)} %bitcast.2, s32[1]{0:T(128)} %bitcast.1, s32[1]{0:T(128)} %bitcast), kind=kLoop, calls=%fused_computation | loop fusion | flops 6 | bytes 24 | tf_op jit(solution)/shard_map/stack | solution.py:348
  1.2 2.0 %pack_rows.1 = (f32[304,128]{1,0:T(8,128)}, f32[304,128]{1,0:T(8,128)}, f32[8,128]{1,0:T(8,128)}) custom-call(s32[3]{0:T(128)} %pad_add_fusion.place, f32[600,128]{1,0:T(8,128)} %bitcast.7, f32[600,128]{1,0:T(8,128)} %bitcast.9, f32[600,128]{1,0:T(8,128)} %bitcast.11, f32[600,128]{1,0:T(8,128)} %bitcast.13, s32[8,128]{1,0:T(8,128)} %refs_7_.1), custom_call_target="tpu_custom_call" | custom-call | tf_op jit(solution)/shard_map/pack_rows/pallas_call | solution.py:355
  3.2 1.9 %collective-permute-start = (f32[304,128]{1,0:T(8,128)}, f32[304,128]{1,0:T(8,128)S(1)}, u32[]{:S(2)}, u32[]{:S(2)}) collective-permute-start(f32[304,128]{1,0:T(8,128)} %get-tuple-element.23.refs_8_), channel_id=1, source_target_pairs={{0,1},{1,0},{2,3},{3,2},{4,5},{5,4},{6,7},{7,6},{8,9},{9,8},{10,11... | collective-permute-start | bytes 466952 | tf_op jit(solution)/shard_map/ppermute | solution.py:361
  5.2 16.1 %collective-permute-start.1 = (f32[304,128]{1,0:T(8,128)}, f32[304,128]{1,0:T(8,128)S(1)}, u32[]{:S(2)}, u32[]{:S(2)}) collective-permute-start(f32[304,128]{1,0:T(8,128)} %get-tuple-element.24.refs_9_), channel_id=1, source_target_pairs={{1,2},{2,1},{3,4},{4,3},{5,6},{6,5},{7,8},{8,7},{9,10},{10,9},{11,... | collective-permute-start | bytes 466952 | tf_op jit(solution)/shard_map/ppermute | solution.py:359
  21.3 0.0 collective-permute-done.refs_5_.refs_10_
  21.3 0.0 copy-start
  21.3 0.7 %copy-done = f32[304,128]{1,0:T(8,128)} copy-done((f32[304,128]{1,0:T(8,128)}, f32[304,128]{1,0:T(8,128)S(1)}, u32[]{:S(2)}) %copy-start) | copy-done | bytes 155672
  21.9 2.7 %pack_columns.1 = (f32[40,128]{1,0:T(8,128)}, f32[40,128]{1,0:T(8,128)}) custom-call(s32[3]{0:T(128)} %pad_add_fusion.place, f32[600,128]{1,0:T(8,128)} %bitcast.8, f32[600,128]{1,0:T(8,128)} %bitcast.10, f32[600,128]{1,0:T(8,128)} %bitcast.12, f32[600,128]{1,0:T(8,128)} %bitcast.14, s32[8,128]{1,0:T(8,128)} %refs_7_.1, f32[304,128]{1,0:T(8,128)} %copy-done), custom_call_target="tpu_custom_call" | custom-call | tf_op jit(solution)/shard_map/pack_columns/pallas_call | solution.py:362
  24.6 3.6 %collective-permute-start.2 = (f32[40,128]{1,0:T(8,128)}, f32[40,128]{1,0:T(8,128)S(1)}, u32[]{:S(2)}, u32[]{:S(2)}) collective-permute-start(f32[40,128]{1,0:T(8,128)} %get-tuple-element.25.refs_12_), channel_id=1, source_target_pairs={{0,16},{16,0},{32,48},{48,32},{64,80},{80,64},{96,112},{112,96},{1... | collective-permute-start | bytes 61448 | tf_op jit(solution)/shard_map/ppermute | solution.py:367
  28.2 7.3 %collective-permute-start.3 = (f32[40,128]{1,0:T(8,128)}, f32[40,128]{1,0:T(8,128)S(1)}, u32[]{:S(2)}, u32[]{:S(2)}) collective-permute-start(f32[40,128]{1,0:T(8,128)} %get-tuple-element.26.refs_13_), channel_id=1, source_target_pairs={{16,32},{32,16},{48,64},{64,48},{80,96},{96,80},{112,128},{128,112... | collective-permute-start | bytes 61448 | tf_op jit(solution)/shard_map/ppermute | solution.py:366
  35.5 0.0 copy-done.5
  35.5 1.9 %collective-permute-start.4 = (f32[8,128]{1,0:T(8,128)S(1)}, f32[8,128]{1,0:T(8,128)S(1)}, u32[]{:S(2)}, u32[]{:S(2)}) collective-permute-start(f32[8,128]{1,0:T(8,128)S(1)} %copy-done.5), channel_id=1, source_target_pairs={{1,498},{498,1},{3,500},{500,3},{5,502},{502,5},{7,504},{504,7},{9... | collective-permute-start | bytes 12296 | tf_op jit(solution)/shard_map/ppermute | solution.py:360
  37.4 7.7 %local_work.1 = (f32[75,8,128]{2,1,0:T(8,128)}, f32[75,8,128]{2,1,0:T(8,128)}, f32[75,8,128]{2,1,0:T(8,128)}, f32[75,8,128]{2,1,0:T(8,128)}, f32[75,8,128]{2,1,0...) custom-call(s32[3]{0:T(128)} %pad_add_fusion.place, f32[75,8,128]{2,1,0:T(8,128)} %refs_0_.1, ...), custom_call_target="tpu_custom_call" | custom-call | tf_op jit(solution)/shard_map/local_work/pallas_call | solution.py:368
  45.1 5.9 %collective-permute-done.4.refs_16_ = f32[8,128]{1,0:T(8,128)S(1)} collective-permute-done((f32[8,128]{1,0:T(8,128)S(1)}, f32[8,128]{1,0:T(8,128)S(1)}, u32[]{:S(2)}, u32[]{:S(2)}) %collective-permute-start.4) | collective-permute-done | bytes 4128 | tf_op jit(solution)/shard_map/ppermute | solution.py:360
  50.9 0.0 collective-permute-done.1.refs_11_
  50.9 0.0 collective-permute-done.2.refs_14_
  50.9 0.0 copy-start.2
  51.0 0.0 collective-permute-done.3.refs_15_
  51.0 0.0 copy-start.3
  51.0 0.5 copy-done.4
  51.5 0.1 copy-done.1
  51.6 0.0 copy-done.2
  51.6 0.0 copy-done.3
  51.6 4.1 %finish.1 = (f32[75,8,128]{2,1,0:T(8,128)}, f32[75,8,128]{2,1,0:T(8,128)}, f32[75,8,128]{2,1,0:T(8,128)}, f32[75,8,128]{2,1,0:T(8,128)}) custom-call(s32[3]{0:T(128)} %pad_add_fusion.place, f32[75,8,128]{2,1,0:T(8,128)} %get-tuple-element.16.refs_0_, f32[75,8,128]{2,1,0:T(8,128)} %get-tuple-element.17.refs_1_, f32[75,8,128]{2,1,0:T(8,128)} %get-tuple-element.18.refs_2_, ...), custom_call_target="tpu_custom_call" | custom-call | tf_op jit(solution)/shard_map/finish/pallas_call | solution.py:372
  (3 shorter events, 0.0 us)
Async XLA Ops:
  3.2 18.0 %collective-permute-start = (f32[304,128]{1,0:T(8,128)}, f32[304,128]{1,0:T(8,128)S(1)}, u32[]{:S(2)}, u32[]{:S(2)}) collective-permute-start(f32[304,128]{1,0:T(8,128)} %get-tuple-element.23.refs_8_), channel_id=1, source_target_pairs={{0,1},{1,0},{2,3},{3,2},{4,5},{5,4},{6,7},{7,6},{8,9},{9,8},{10,11... | collective-permute-start | bytes 466952 | tf_op jit(solution)/shard_map/ppermute | solution.py:361
  5.2 45.8 %collective-permute-start.1 = (f32[304,128]{1,0:T(8,128)}, f32[304,128]{1,0:T(8,128)S(1)}, u32[]{:S(2)}, u32[]{:S(2)}) collective-permute-start(f32[304,128]{1,0:T(8,128)} %get-tuple-element.24.refs_9_), channel_id=1, source_target_pairs={{1,2},{2,1},{3,4},{4,3},{5,6},{6,5},{7,8},{8,7},{9,10},{10,9},{11,... | collective-permute-start | bytes 466952 | tf_op jit(solution)/shard_map/ppermute | solution.py:359
  21.3 0.7 %copy-start = (f32[304,128]{1,0:T(8,128)}, f32[304,128]{1,0:T(8,128)S(1)}, u32[]{:S(2)}) copy-start(f32[304,128]{1,0:T(8,128)S(1)} %collective-permute-done.refs_5_.refs_10_) | copy-start | bytes 466948
  24.6 10.9 %copy-start.5 = (f32[8,128]{1,0:T(8,128)S(1)}, f32[8,128]{1,0:T(8,128)}, u32[]{:S(2)}) copy-start(f32[8,128]{1,0:T(8,128)} %get-tuple-element.27) | copy-start | bytes 12292
  24.6 26.4 %collective-permute-start.2 = (f32[40,128]{1,0:T(8,128)}, f32[40,128]{1,0:T(8,128)S(1)}, u32[]{:S(2)}, u32[]{:S(2)}) collective-permute-start(f32[40,128]{1,0:T(8,128)} %get-tuple-element.25.refs_12_), channel_id=1, source_target_pairs={{0,16},{16,0},{32,48},{48,32},{64,80},{80,64},{96,112},{112,96},{1... | collective-permute-start | bytes 61448 | tf_op jit(solution)/shard_map/ppermute | solution.py:367
  28.2 22.8 %collective-permute-start.3 = (f32[40,128]{1,0:T(8,128)}, f32[40,128]{1,0:T(8,128)S(1)}, u32[]{:S(2)}, u32[]{:S(2)}) collective-permute-start(f32[40,128]{1,0:T(8,128)} %get-tuple-element.26.refs_13_), channel_id=1, source_target_pairs={{16,32},{32,16},{48,64},{64,48},{80,96},{96,80},{112,128},{128,112... | collective-permute-start | bytes 61448 | tf_op jit(solution)/shard_map/ppermute | solution.py:366
  35.5 15.4 %collective-permute-start.4 = (f32[8,128]{1,0:T(8,128)S(1)}, f32[8,128]{1,0:T(8,128)S(1)}, u32[]{:S(2)}, u32[]{:S(2)}) collective-permute-start(f32[8,128]{1,0:T(8,128)S(1)} %copy-done.5), channel_id=1, source_target_pairs={{1,498},{498,1},{3,500},{500,3},{5,502},{502,5},{7,504},{504,7},{9... | collective-permute-start | bytes 12296 | tf_op jit(solution)/shard_map/ppermute | solution.py:360
  50.9 0.6 %copy-start.4 = (f32[8,128]{1,0:T(8,128)}, f32[8,128]{1,0:T(8,128)S(1)}, u32[]{:S(2)}) copy-start(f32[8,128]{1,0:T(8,128)S(1)} %collective-permute-done.4.refs_16_) | copy-start | bytes 12292
  50.9 0.7 %copy-start.1 = (f32[304,128]{1,0:T(8,128)}, f32[304,128]{1,0:T(8,128)S(1)}, u32[]{:S(2)}) copy-start(f32[304,128]{1,0:T(8,128)S(1)} %collective-permute-done.1.refs_11_) | copy-start | bytes 466948
  50.9 0.7 %copy-start.2 = (f32[40,128]{1,0:T(8,128)}, f32[40,128]{1,0:T(8,128)S(1)}, u32[]{:S(2)}) copy-start(f32[40,128]{1,0:T(8,128)S(1)} %collective-permute-done.2.refs_14_) | copy-start | bytes 61444
  51.0 0.6 %copy-start.3 = (f32[40,128]{1,0:T(8,128)}, f32[40,128]{1,0:T(8,128)S(1)}, u32[]{:S(2)}) copy-start(f32[40,128]{1,0:T(8,128)S(1)} %collective-permute-done.3.refs_15_) | copy-start | bytes 61444

commit v2 on v1

v2 whole, which is shorter than its diff:
```python
import jax
import jax.numpy as jnp
from jax import lax
from jax.experimental import pallas as pl
from jax.experimental.pallas import tpu as pltpu
from jax.sharding import PartitionSpec as P


DT = 0.2
CORIOLIS = 1.5
PRESSURE = 0.05
VISC_STEP = 0.1

ROWS, LANES = 8, 128
VMEM_GRANT = 8 << 20
COL_ROWS = 40


def elimination_constants(levels):
    inner, last = [], []
    for k in range(levels):
        above = VISC_STEP * VISC_STEP * inner[k - 1] if k else 0.0
        step = VISC_STEP if k else 0.0
        inner.append(1.0 / (1.0 + step + VISC_STEP - above))
        last.append(1.0 / (1.0 + step - above))
    return inner, last


def lane_ids():
    return lax.broadcasted_iota(jnp.int32, (ROWS, LANES), 1)


def row_ids():
    return lax.broadcasted_iota(jnp.int32, (ROWS, LANES), 0)


def roll(x, shift, axis):
    return pltpu.roll(x, shift % x.shape[axis], axis)


def density_of(t, s):
    return -(1.0 + 0.1 * t) * t + 0.8 * s - 0.1 * t * s


def level_to_lane(rows, lane):
    k = lax.broadcasted_iota(jnp.int32, rows.shape, 0)
    l = lax.broadcasted_iota(jnp.int32, rows.shape, 1)
    return jnp.sum(jnp.where(k == l, rows[:, lane : lane + 1], 0.0), axis=0, keepdims=True)


def place_of(n_lat, n_lon):
    lat, lon = lax.axis_index("lat"), lax.axis_index("lon")
    return lat, lon, lax.rem(lat, 4) < 2, lat == n_lat - 1, lon == n_lon - 1


def pack_rows(mesh_size, levels, t, s, u, v, depth, t_out, s_out, u_out, v_out, h_out, to_a, to_b, corner, ints, sems):
    lat, _, _, _, _ = place_of(*mesh_size)
    even = lax.rem(lat, 2) == 0
    outs = (t_out, s_out, u_out, v_out)
    copies = [
        pltpu.make_async_copy(x, y, sems.at[f]) for f, (x, y) in enumerate(zip((t, s, u, v), outs))
    ]
    copies.append(pltpu.make_async_copy(depth, ints, sems.at[4]))
    for copy in copies:
        copy.start()
    copies[4].wait()
    h = ints[...].astype(jnp.float32)
    h_out[...] = h
    blank = jnp.zeros((3, LANES), jnp.float32)
    last = 4 * levels
    to_a[last : last + 4, :] = jnp.concatenate([jnp.where(even, h[7:8], h[0:1]), blank], axis=0)
    to_b[last : last + 4, :] = jnp.concatenate([jnp.where(even, h[0:1], h[7:8]), blank], axis=0)
    packed = []
    for f, ref in enumerate(outs):
        copies[f].wait()
        top = ref[pl.ds(ROWS - 1, levels, stride=ROWS), :]
        low = ref[pl.ds(0, levels, stride=ROWS), :]
        to_a[pl.ds(f, levels, stride=4), :] = jnp.where(even, top, low)
        b = jnp.where(even, low, top)
        to_b[pl.ds(f, levels, stride=4), :] = b
        packed.append(b)
    cu = level_to_lane(packed[2], LANES - 1)
    cv = level_to_lane(packed[3], 0)
    row = row_ids()
    corner[...] = jnp.where(row == 0, cu, jnp.where(row == 1, cv, 0.0))


def pack_columns(mesh_size, levels, early, t, s, u, v, depth, from_a, *refs):
    to_c, to_d = refs[-2:]
    lat, lon, first, _, _ = place_of(*mesh_size)
    lat_even = lax.rem(lat, 2) == 0
    lon_even = lax.rem(lon, 2) == 0
    if not early:

        @pl.when(first)
        def _():
            to_c[...] = refs[0][...]
            to_d[...] = refs[1][...]

    @pl.when(first if early else jnp.logical_not(first))
    def _():
        lane = lane_ids()
        h = depth[...]
        for f, ref in enumerate((t, s, u, v)):
            east = jnp.zeros((ROWS, LANES), jnp.float32)
            west = jnp.zeros((ROWS, LANES), jnp.float32)
            for k in range(levels):
                x = ref[k * ROWS : (k + 1) * ROWS, :]
                east = jnp.where(lane == k, x[:, LANES - 1 : LANES], east)
                west = jnp.where(lane == k, x[:, 0:1], west)
            if f == 0:
                east = jnp.where(lane == levels, h[:, LANES - 1 : LANES], east)
                west = jnp.where(lane == levels, h[:, 0:1], west)
            to_c[f * ROWS : (f + 1) * ROWS, :] = jnp.where(lon_even, east, west)
            to_d[f * ROWS : (f + 1) * ROWS, :] = jnp.where(lon_even, west, east)
        cu = level_to_lane(from_a[pl.ds(2, levels, stride=4), :], LANES - 1)
        cv = level_to_lane(from_a[pl.ds(3, levels, stride=4), :], 0)
        east = jnp.broadcast_to(jnp.where(lat_even, cu, 0.0), (ROWS, LANES))
        west = jnp.broadcast_to(jnp.where(lat_even, 0.0, cv), (ROWS, LANES))
        to_c[4 * ROWS : 5 * ROWS, :] = jnp.where(lon_even, east, west)
        to_d[4 * ROWS : 5 * ROWS, :] = jnp.where(lon_even, west, east)


def coriolis_rows(lat, total):
    row = (lat * ROWS + row_ids()).astype(jnp.float32)
    return CORIOLIS * (2.0 * (row + 0.5) / total - 1.0)


def local_work(mesh_size, levels, total, early, *refs):
    t, s, u, v, mix, depth = refs[:6]
    st, ss, su, sv, ra, aa, ba = refs[-7:]
    lat, _, first, _, _ = place_of(*mesh_size)

    @pl.when(first if early else jnp.logical_not(first))
    def _():
        lane, row = lane_ids(), row_ids()
        h = depth[...]
        f4 = (0.25 * DT) * coriolis_rows(lat, total)
        open_e = jnp.where(lane < LANES - 1, jnp.minimum(h, roll(h, -1, 1)), 0.0)
        open_n = jnp.where(row < ROWS - 1, jnp.minimum(h, roll(h, -1, 0)), 0.0)
        zero = jnp.zeros((ROWS, LANES), jnp.float32)
        one = jnp.ones((ROWS, LANES), jnp.float32)
        summed, c_here = zero, zero
        minor, minor_prev = one, zero
        for k in range(levels):
            at = slice(k * ROWS, (k + 1) * ROWS)
            tk, sk, uk, vk = t[at, :], s[at, :], u[at, :], v[at, :]
            wet = h > float(k)
            dens = jnp.where(wet, PRESSURE * density_of(tk, sk), 0.0)
            summed = summed + dens
            p = summed - 0.5 * dens
            me, mn = open_e > float(k), open_n > float(k)
            half_u, half_v = 0.5 * uk, 0.5 * vk
            e0, e1 = jnp.where(me, half_u + 0.5, 0.0), jnp.where(me, half_u - 0.5, 0.0)
            n0, n1 = jnp.where(mn, half_v + 0.5, 0.0), jnp.where(mn, half_v - 0.5, 0.0)
            for x, out in ((tk, st), (sk, ss)):
                fe = e0 * x + e1 * roll(x, -1, 1)
                fn = n0 * x + n1 * roll(x, -1, 0)
                out[k] = x - DT * (fe - roll(fe, 1, 1) + fn - roll(fn, 1, 0))
            uw, ve = roll(uk, 1, 1), roll(vk, -1, 1)
            un, vs = roll(uk, -1, 0), roll(vk, 1, 0)
            lap_u = (roll(uk, -1, 1) + uw) + (un + roll(uk, 1, 0)) - 4.0 * uk
            lap_v = (ve + roll(vk, 1, 1)) + (roll(vk, -1, 0) + vs) - 4.0 * vk
            v4 = (vk + ve) + (vs + roll(ve, 1, 0))
            u4 = (uk + uw) + (un + roll(uw, -1, 0))
            su[k] = uk + f4 * v4 - DT * (roll(p, -1, 1) - p) + 0.1 * lap_u
            sv[k] = vk - f4 * u4 - DT * (roll(p, -1, 0) - p) + 0.1 * lap_v
            c_next = jnp.where(h > float(k + 1), DT * mix[k], 0.0) if k < levels - 1 else zero
            minor_next = (1.0 + c_here + c_next) * minor - (c_here * c_here) * minor_prev
            r = jnp.where(wet, minor / minor_next, 0.0)
            minor_prev, minor = minor, minor_next
            ra[k] = r
            aa[k] = c_here * r
            ba[k] = c_next * r
            c_here = c_next


def finish(mesh_size, levels, total, *refs):
    (st, ss, su, sv, ra, aa, ba, depth, to_a, to_b, a_p, a_q, b_p, b_q, c_own, d_own,
     c_p, d_p, c_q, d_q, corner_p, corner_q, ot, os, ou, ov, north, south, kept) = refs
    lat, lon, first, top, lon_last = place_of(*mesh_size)
    lane, row = lane_ids(), row_ids()
    lat_even = lax.rem(lat, 2) == 0
    lon_even = lax.rem(lon, 2) == 0
    b_first = jnp.logical_or(first, top)
    d_first = jnp.logical_and(first, jnp.logical_not(lon_last))
    h = depth[...]
    f4 = (0.25 * DT) * coriolis_rows(lat, total)
    f7, f0 = f4[7:8, :], f4[0:1, :]

    kk = lax.broadcasted_iota(jnp.int32, (levels, LANES), 0).astype(jnp.float32)
    ll = lax.broadcasted_iota(jnp.int32, (levels, LANES), 1)

    def field(ref, f):
        return ref[pl.ds(f, levels, stride=4), :]

    def ghosts(f):
        a = jnp.where(first, field(a_p, f), field(a_q, f))
        b = jnp.where(b_first, field(b_p, f), field(b_q, f))
        return jnp.where(lat_even, a, b), jnp.where(lat_even, b, a)

    def own(f):
        a, b = field(to_a, f), field(to_b, f)
        return jnp.where(lat_even, a, b), jnp.where(lat_even, b, a)

    def mirrored(x, last):
        ids = lax.rem(last + LANES - lax.broadcasted_iota(jnp.int32, x.shape, 1), LANES)
        return jnp.take_along_axis(x, ids, axis=1)

    at = slice(4 * levels, 4 * levels + 1)
    h_a = jnp.where(first, a_p[at, :], a_q[at, :])
    h_b = jnp.where(b_first, b_p[at, :], b_q[at, :])
    h_n = jnp.broadcast_to(jnp.where(lat_even, h_a, h_b), (ROWS, LANES))
    h_n = jnp.where(top, mirrored(h_n, LANES - 1), h_n)[0:1, :]
    h_s = jnp.where(lat_even, h_b, h_a)
    (tn, ts), (sn, ss_), (un, us), (vn, vs) = (ghosts(f) for f in range(4))
    (t7, t0), (s7, s0), (u7, u0), (v7, v0) = (own(f) for f in range(4))
    tn = jnp.where(top, mirrored(tn, LANES - 1), tn)
    sn = jnp.where(top, mirrored(sn, LANES - 1), sn)
    vn = jnp.where(top, -mirrored(vn, LANES - 1), vn)
    un = jnp.where(top, -mirrored(un, LANES - 2), un)
    unw = roll(un, 1, 1)
    unw = jnp.where(ll > 0, unw - roll(u0, 1, 1), jnp.where(top, unw, 0.0))
    un = jnp.where(jnp.logical_and(top, ll == LANES - 1), 0.0, un) - u0
    mask = jnp.minimum(h[7:8, :], h_n) > kk
    north[0, :levels, :] = jnp.where(mask, -0.1 * (v7 * (t7 + tn) - (tn - t7)), 0.0)
    north[1, :levels, :] = jnp.where(mask, -0.1 * (v7 * (s7 + sn) - (sn - s7)), 0.0)
    north[2, :levels, :] = 0.1 * un
    north[3, :levels, :] = 0.1 * (vn - v0) - f7 * (un + unw)
    north[4, :levels, :] = (DT * PRESSURE) * (
        jnp.where(h_n > kk, density_of(tn, sn), 0.0)
        - jnp.where(h[0:1, :] > kk, density_of(t0, s0), 0.0)
    )
    mask = jnp.minimum(h[0:1, :], h_s) > kk
    south[0, :levels, :] = jnp.where(mask, 0.1 * (vs * (ts + t0) - (t0 - ts)), 0.0)
    south[1, :levels, :] = jnp.where(mask, 0.1 * (vs * (ss_ + s0) - (s0 - ss_)), 0.0)
    vs = vs - v7
    vse = jnp.where(ll < LANES - 1, roll(vs, -1, 1), 0.0)
    south[2, :levels, :] = 0.1 * (us - u7) + f0 * (vs + vse)
    south[3, :levels, :] = 0.1 * vs

    kl = lane.astype(jnp.float32)

    def tiles(c, d, f):
        at = slice(f * ROWS, (f + 1) * ROWS)
        x = jnp.where(first, c[0][at, :], c[1][at, :])
        y = jnp.where(d[2], d[0][at, :], d[1][at, :])
        return jnp.where(lon_even, x, y), jnp.where(lon_even, y, x)

    got_c, got_d = (c_p, c_q), (d_p, d_q, d_first)
    own_c, own_d = (c_own, c_own), (d_own, d_own, first)
    (te, tw), (se, sw), (ue, uw), (ve, vw), (ce, cw) = (tiles(got_c, got_d, f) for f in range(5))
    (t9, tz), (s9, sz), (u9, uz), (v9, vz) = (tiles(own_c, own_d, f) for f in range(4))
    cb = jnp.where(b_first, corner_p[...], corner_q[...])
    cb_u = jnp.broadcast_to(cb[0:1, :], (ROWS, LANES))
    cb_v = jnp.broadcast_to(cb[1:2, :], (ROWS, LANES))
    south_east = jnp.where(lat_even, cb_v, ce)
    north_west = jnp.where(lat_even, cw, jnp.where(top, 0.0, cb_u))
    north_end = jnp.where(jnp.logical_and(top, row == ROWS - 1), -cb_u, 0.0)
    h_e = te[:, levels : levels + 1]
    h_w = tw[:, levels : levels + 1]
    mask = jnp.minimum(h[:, LANES - 1 : LANES], h_e) > kl
    dt_e = jnp.where(mask, -0.1 * (u9 * (t9 + te) - (te - t9)), 0.0)
    ds_e = jnp.where(mask, -0.1 * (u9 * (s9 + se) - (se - s9)), 0.0)
    mask = jnp.minimum(h[:, 0:1], h_w) > kl
    dt_w = jnp.where(mask, 0.1 * (uw * (tw + tz) - (tz - tw)), 0.0)
    ds_w = jnp.where(mask, 0.1 * (uw * (sw + sz) - (sz - sw)), 0.0)
    dens = jnp.where(h_e > kl, density_of(te, se), 0.0) - jnp.where(
        h[:, 0:1] > kl, density_of(tz, sz), 0.0
    )
    summed = dens
    for step in (1, 2, 4, 8, 16, 32, 64):
        summed = summed + jnp.where(lane >= step, roll(summed, step, 1), 0.0)
    pe = (DT * PRESSURE) * (summed - 0.5 * dens)
    ve_up = jnp.where(row > 0, roll(ve, 1, 0), south_east) - roll(vz, 1, 0)
    uw_dn = jnp.where(row < ROWS - 1, roll(uw, -1, 0), north_west) - roll(u9, -1, 0)
    du_e = f4 * ((ve - vz) + ve_up) - pe + 0.1 * (ue - uz) + 0.1 * north_end
    du_w = 0.1 * (uw - u9)
    dv_e = 0.1 * (ve - vz) - f4 * north_end
    dv_w = 0.1 * (vw - v9) - f4 * ((uw - u9) + uw_dn)

    m_u = jnp.minimum(h, jnp.where(lane < LANES - 1, roll(h, -1, 1), h_e))
    m_v = jnp.minimum(h, jnp.where(row < ROWS - 1, roll(h, -1, 0), h_n))
    at_n, at_s = row == ROWS - 1, row == 0
    at_e, at_w = lane == LANES - 1, lane == 0
    inner, last = elimination_constants(levels)
    pt = ps = pu = pv = jnp.zeros((ROWS, LANES), jnp.float32)
    cs = jnp.zeros((1, LANES), jnp.float32)
    for k in range(levels):

        def spread(f, de, dw, extra=None):
            n = north[f, k : k + 1, :]
            if extra is not None:
                n = n - extra
            base = jnp.where(at_n, n, jnp.where(at_s, south[f, k : k + 1, :], 0.0))
            side = jnp.where(at_e, de[:, k : k + 1], jnp.where(at_w, dw[:, k : k + 1], 0.0))
            return base + side

        dn = north[4, k : k + 1, :]
        cs = cs + dn
        r, a = ra[k], aa[k]
        pt = r * (st[k] + spread(0, dt_e, dt_w)) + a * pt
        ps = r * (ss[k] + spread(1, ds_e, ds_w)) + a * ps
        ru = jnp.where(m_u > float(k + 1), inner[k], jnp.where(m_u > float(k), last[k], 0.0))
        rv = jnp.where(m_v > float(k + 1), inner[k], jnp.where(m_v > float(k), last[k], 0.0))
        pu = ru * (su[k] + spread(2, du_e, du_w)) + (VISC_STEP * ru) * pu
        pv = rv * (sv[k] + spread(3, dv_e, dv_w, cs - 0.5 * dn)) + (VISC_STEP * rv) * pv
        kept[0, k] = pt
        kept[1, k] = ps
        kept[2, k] = pu
        kept[3, k] = pv
    xt, xs, xu, xv = pt, ps, pu, pv
    for k in range(levels - 1, -1, -1):
        if k < levels - 1:
            b = ba[k]
            bu = jnp.where(m_u > float(k + 1), VISC_STEP * inner[k], 0.0)
            bv = jnp.where(m_v > float(k + 1), VISC_STEP * inner[k], 0.0)
            xt = kept[0, k] + b * xt
            xs = kept[1, k] + b * xs
            xu = kept[2, k] + bu * xu
            xv = kept[3, k] + bv * xv
        ot[k] = xt
        os[k] = xs
        ou[k] = xu
        ov[k] = xv


HBM = pl.BlockSpec(memory_space=pltpu.HBM)
VMEM = pl.BlockSpec(memory_space=pltpu.VMEM)


def call(body, far, near, outs, scratch=(), aliases=None, keep=True):
    far = [pltpu.with_memory_space_constraint(x, pltpu.HBM) for x in far]
    near = [pltpu.with_memory_space_constraint(x, pltpu.VMEM) for x in near]
    shapes = tuple(
        pltpu.VMEM(s, jnp.float32) if keep else jax.ShapeDtypeStruct(s, jnp.float32) for s in outs
    )
    return pl.pallas_call(
        body,
        out_shape=shapes,
        in_specs=[HBM] * len(far) + [VMEM] * len(near),
        out_specs=tuple(VMEM for _ in outs),
        scratch_shapes=list(scratch),
        input_output_aliases=aliases or {},
        compiler_params=pltpu.CompilerParams(vmem_limit_bytes=VMEM_GRANT),
    )(*far, *near)


def exchanges(n_lat, n_lon):
    def at(lat, lon):
        return (lon % n_lon) * n_lat + lat

    def both(x, y):
        return [(x, y), (y, x)]

    p = {name: [] for name in [x + y for x in "abkcd" for y in ("_p", "_q")]}
    for lon in range(n_lon):
        for lat in range(0, n_lat, 2):
            p["a_p" if lat % 4 < 2 else "a_q"] += both(at(lat, lon), at(lat + 1, lon))
        for lat in range(1, n_lat - 1, 2):
            for x, y in both((lat, lon), (lat + 1, lon)):
                p["b_p" if y[0] % 4 < 2 else "b_q"].append((at(*x), at(*y)))
            for x, y in both((lat, lon), (lat + 1, lon - 1)):
                p["k_p" if y[0] % 4 < 2 else "k_q"].append((at(*x), at(*y)))
        p["b_p"].append((at(n_lat - 1, lon), at(n_lat - 1, n_lon - 1 - lon)))
        p["k_p"].append((at(n_lat - 1, lon), at(n_lat - 1, n_lon - 2 - lon)))
    for lat in range(n_lat):
        side = "p" if lat % 4 < 2 else "q"
        for lon in range(0, n_lon, 2):
            p["c_" + side] += both(at(lat, lon), at(lat, lon + 1))
            p["d_" + side].append((at(lat, lon + 1), at(lat, lon + 2)))
            wraps = lon + 2 == n_lon
            p["d_q" if wraps else "d_" + side].append((at(lat, lon + 2), at(lat, lon + 1)))
    return p


def local(t, s, u, v, mix, depth):
    levels = t.shape[0]
    size = (lax.axis_size("lat"), lax.axis_size("lon"))
    total = float(size[0] * ROWS)
    pairs = exchanges(*size)
    flat = (levels * ROWS, LANES)
    rows, full = (4 * levels + 4, LANES), (levels, ROWS, LANES)
    column = (COL_ROWS, LANES)

    def send(x, name):
        return lax.ppermute(x, ("lon", "lat"), pairs[name])

    def bind(body, *args):
        return lambda *refs: body(size, levels, *args, *refs)

    *fields, depth, to_a, to_b, to_corner = call(
        bind(pack_rows), [x.reshape(flat) for x in (t, s, u, v)] + [depth], [],
        [flat] * 4 + [(ROWS, LANES), rows, rows, (ROWS, LANES)],
        [pltpu.VMEM((ROWS, LANES), jnp.int32), pltpu.SemaphoreType.DMA((5,))],
    )
    b_p = send(to_b, "b_p")
    k_p = send(to_corner, "k_p")
    a_p = send(to_a, "a_p")
    cols_p = call(bind(pack_columns, True), [], [*fields, depth, a_p], [column] * 2)
    d_p = send(cols_p[1], "d_p")
    c_p = send(cols_p[0], "c_p")
    work = call(bind(local_work, total, True), [], [*fields, mix, depth], [full] * 7)
    b_q = send(to_b, "b_q")
    k_q = send(to_corner, "k_q")
    a_q = send(to_a, "a_q")
    cols_q = call(bind(pack_columns, False), [], [*fields, depth, a_q, *cols_p], [column] * 2)
    d_q = send(cols_q[1], "d_q")
    c_q = send(cols_q[0], "c_q")
    work = call(
        bind(local_work, total, False), [], [*fields, mix, depth, *work], [full] * 7,
        aliases={6 + i: i for i in range(7)},
    )
    padded = (levels + 7) // 8 * 8
    return tuple(
        call(
            bind(finish, total), [],
            [*work, depth, to_a, to_b, a_p, a_q, b_p, b_q, *cols_q, c_p, d_p, c_q, d_q, k_p, k_q],
            [full] * 4,
            [
                pltpu.VMEM((5, padded, LANES), jnp.float32),
                pltpu.VMEM((4, padded, LANES), jnp.float32),
                pltpu.VMEM((4,) + full, jnp.float32),
            ],
            keep=False,
        )
    )


def solution(mesh):
    field = P(None, "lat", "lon")

    return jax.shard_map(
        local,
        mesh=mesh,
        in_specs=(field,) * 5 + (P("lat", "lon"),),
        out_specs=(field,) * 4,
        check_vma=False,
    )
```

time: 56.1 us -> 65.9 us (1.17)
  starting transfers between devices: 30.8 us -> 54.9 us
  Pallas kernels: 16.5 us -> 9.81 us
  waiting for transfers between devices: 5.87 us -> 0.03 us
  local copies, waits for them, and re-layouts: 1.31 us -> 0.01 us
    ppermute x5 -> x10, starting transfers between devices: 30.8 us -> 54.9 us  [send(): return lax.ppermute(x, ('lon', 'lat'), pairs[name])]
    pallas_call x4 -> x6, Pallas kernels: 16.5 us -> 9.81 us  [call(): pl.pallas_call(body, out_shape=shapes, in_specs=[HBM] * len(far) + [VMEM]...]
    ppermute x5 -> x10, waiting for transfers between devices: 5.87 us -> 0.03 us  [send(): return lax.ppermute(x, ('lon', 'lat'), pairs[name])]
    unnamed x12 -> x2, local copies, waits for them, and re-layouts: 1.31 us -> 0.01 us
  transfers between devices with their start and end apart: 5 -> 10, of which waited for: 1 -> 0; matrix products, arithmetic and copies ran while one was open for 0% -> 0% of each run, Pallas kernels for 19% -> 9%
where the time goes in v2:
time: 65.9 us; the launch traced here: 65.6 us
  starting transfers between devices  54.9 us (83%)
  Pallas kernels  9.81 us (15%)
  between operations  0.84 us (1%)
    ppermute x10, starting transfers between devices, send(): return lax.ppermute(x, ('lon', 'lat'), pairs[name])  54.9 us
    pallas_call x6, Pallas kernels, call(): pl.pallas_call(body, out_shape=shapes, in_specs=[HBM] * len(far) + [VMEM]...  9.81 us
  transfers between devices with their start and end apart: 10, of which 0 were waited for; matrix products, arithmetic and copies ran while one was open for 0% of the time, Pallas kernels for 9%

profile of v2, /device:TPU:6, one launch (start us, length us, event | category | flops | bytes accessed | tf_op | source)
XLA Modules:
  0.0 65.6 jit_solution(12367492260329523728)
XLA Ops:
  0.6 1.4 %shard_map.93 = (f32[600,128]{1,0:T(8,128)S(1)}, f32[600,128]{1,0:T(8,128)S(1)}, f32[600,128]{1,0:T(8,128)S(1)}, f32[600,128]{1,0:T(8,128)S(1)}, f32[8,128]{1,0:...) custom-call(f32[600,128]{1,0:T(8,128)} %bitcast.4, f32[600,128]{1,0:T(8,128)} %bitcast.5, ...), custom_call_target="tpu_custom_call" | custom-call | tf_op jit(solution)/shard_map/pallas_call | solution.py:338
  2.0 1.9 %collective-permute-start = (f32[304,128]{1,0:T(8,128)S(1)}, f32[304,128]{1,0:T(8,128)S(1)}, u32[]{:S(2)}, u32[]{:S(2)}) collective-permute-start(f32[304,128]{1,0:T(8,128)S(1)} %get-tuple-element.49.refs_8_), channel_id=1, source_target_pairs={{0,1},{1,0},{4,5},{5,4},{8,9},{9,8},{12,13},{13,12},{16,17},{17,16... | collective-permute-start | bytes 466952 | tf_op jit(solution)/shard_map/ppermute | solution.py:387
  4.0 0.7 %collective-permute-start.1 = (f32[304,128]{1,0:T(8,128)S(1)}, f32[304,128]{1,0:T(8,128)S(1)}, u32[]{:S(2)}, u32[]{:S(2)}) collective-permute-start(f32[304,128]{1,0:T(8,128)S(1)} %get-tuple-element.49.refs_8_), channel_id=1, source_target_pairs={{2,3},{3,2},{6,7},{7,6},{10,11},{11,10},{14,15},{15,14},{18,19},{1... | collective-permute-start | bytes 466952 | tf_op jit(solution)/shard_map/ppermute | solution.py:387
  4.6 1.3 %collective-permute-start.2 = (f32[304,128]{1,0:T(8,128)S(1)}, f32[304,128]{1,0:T(8,128)S(1)}, u32[]{:S(2)}, u32[]{:S(2)}) collective-permute-start(f32[304,128]{1,0:T(8,128)S(1)} %get-tuple-element.50.refs_9_), channel_id=1, source_target_pairs={{2,1},{3,4},{6,5},{7,8},{10,9},{11,12},{14,13},{15,511},{18,17},{1... | collective-permute-start | bytes 466952 | tf_op jit(solution)/shard_map/ppermute | solution.py:387
  5.9 16.1 %collective-permute-start.3 = (f32[304,128]{1,0:T(8,128)S(1)}, f32[304,128]{1,0:T(8,128)S(1)}, u32[]{:S(2)}, u32[]{:S(2)}) collective-permute-start(f32[304,128]{1,0:T(8,128)S(1)} %get-tuple-element.50.refs_9_), channel_id=1, source_target_pairs={{1,2},{4,3},{5,6},{8,7},{9,10},{12,11},{13,14},{17,18},{20,19},{21... | collective-permute-start | bytes 466952 | tf_op jit(solution)/shard_map/ppermute | solution.py:387
  22.0 1.3 %collective-permute-start.8 = (f32[8,128]{1,0:T(8,128)S(1)}, f32[8,128]{1,0:T(8,128)S(1)}, u32[]{:S(2)}, u32[]{:S(2)}) collective-permute-start(f32[8,128]{1,0:T(8,128)S(1)} %get-tuple-element.55), channel_id=1, source_target_pairs={{498,1},{3,500},{502,5},{7,504},{506,9},{11,508},{510,13},{15,495}... | collective-permute-start | bytes 12296 | tf_op jit(solution)/shard_map/ppermute | solution.py:387
  23.3 0.0 collective-permute-done.refs_5_.refs_10_
  23.4 14.8 %collective-permute-start.9 = (f32[8,128]{1,0:T(8,128)S(1)}, f32[8,128]{1,0:T(8,128)S(1)}, u32[]{:S(2)}, u32[]{:S(2)}) collective-permute-start(f32[8,128]{1,0:T(8,128)S(1)} %get-tuple-element.55), channel_id=1, source_target_pairs={{1,498},{500,3},{5,502},{504,7},{9,506},{508,11},{13,510},{17,2},{... | collective-permute-start | bytes 12296 | tf_op jit(solution)/shard_map/ppermute | solution.py:387
  38.1 0.7 %shard_map.96 = (f32[40,128]{1,0:T(8,128)S(1)}, f32[40,128]{1,0:T(8,128)S(1)}) custom-call(f32[600,128]{1,0:T(8,128)S(1)} %get-tuple-element.30.refs_0_, f32[600,128]{1,0:T(8,128)S(1)} %get-tuple-element.31.refs_1_, f32[600,128]{1,0:T(8,128)S(1)} %get-tuple-element.32.refs_2_, f32[600,128]{1,0:T(8,128)S(1)} %get-tuple-element.33.refs_3_, ...), custom_call_target="tpu_custom_call" | custom-call | tf_op jit(solution)/shard_map/pallas_call | solution.py:338
  38.9 0.0 collective-permute-done.1.refs_5_.refs_11_
  38.9 3.5 %collective-permute-start.4 = (f32[40,128]{1,0:T(8,128)S(1)}, f32[40,128]{1,0:T(8,128)S(1)}, u32[]{:S(2)}, u32[]{:S(2)}) collective-permute-start(f32[40,128]{1,0:T(8,128)S(1)} %get-tuple-element.51.refs_6_), channel_id=1, source_target_pairs={{0,16},{16,0},{32,48},{48,32},{64,80},{80,64},{96,112},{112,96},{1... | collective-permute-start | bytes 61448 | tf_op jit(solution)/shard_map/ppermute | solution.py:387
  42.4 0.0 copy-start
  42.4 0.0 collective-permute-done.8.refs_20_
  42.5 1.4 %collective-permute-start.5 = (f32[40,128]{1,0:T(8,128)S(1)}, f32[40,128]{1,0:T(8,128)S(1)}, u32[]{:S(2)}, u32[]{:S(2)}) collective-permute-start(f32[40,128]{1,0:T(8,128)S(1)} %get-tuple-element.52.refs_7_), channel_id=1, source_target_pairs={{16,32},{32,16},{48,64},{64,48},{80,96},{96,80},{112,128},{128,112... | collective-permute-start | bytes 61448 | tf_op jit(solution)/shard_map/ppermute | solution.py:387
  43.9 0.0 collective-permute-done.9.refs_21_
  43.9 0.7 %collective-permute-start.6 = (f32[40,128]{1,0:T(8,128)S(1)}, f32[40,128]{1,0:T(8,128)S(1)}, u32[]{:S(2)}, u32[]{:S(2)}) collective-permute-start(f32[40,128]{1,0:T(8,128)S(1)} %get-tuple-element.53.refs_14_), channel_id=1, source_target_pairs={{2,18},{18,2},{34,50},{50,34},{66,82},{82,66},{98,114},{114,98},{1... | collective-permute-start | bytes 61448 | tf_op jit(solution)/shard_map/ppermute | solution.py:387
  44.6 0.0 collective-permute-done.2.refs_12_
  44.6 13.3 %collective-permute-start.7 = (f32[40,128]{1,0:T(8,128)S(1)}, f32[40,128]{1,0:T(8,128)S(1)}, u32[]{:S(2)}, u32[]{:S(2)}) collective-permute-start(f32[40,128]{1,0:T(8,128)S(1)} %get-tuple-element.54.refs_15_), channel_id=1, source_target_pairs={{0,496},{1,497},{18,34},{34,18},{50,66},{66,50},{82,98},{98,82},{1... | collective-permute-start | bytes 61448 | tf_op jit(solution)/shard_map/ppermute | solution.py:387
  57.9 4.9 %shard_map.94 = (f32[75,8,128]{2,1,0:T(8,128)S(1)}, f32[75,8,128]{2,1,0:T(8,128)S(1)}, f32[75,8,128]{2,1,0:T(8,128)S(1)}, f32[75,8,128]{2,1,0:T(8,128)S(1)}, f32...) custom-call(f32[600,128]{1,0:T(8,128)S(1)} %get-tuple-element.30.refs_0_, ...), custom_call_target="tpu_custom_call" | custom-call | tf_op jit(solution)/shard_map/pallas_call | solution.py:338
  62.8 0.0 collective-permute-done.3.refs_13_
  62.8 0.0 collective-permute-done.4.refs_16_
  62.9 0.0 collective-permute-done.6.refs_18_
  62.9 0.0 collective-permute-done.7.refs_19_
  62.9 2.7 %shard_map.98 = (f32[75,8,128]{2,1,0:T(8,128)}, f32[75,8,128]{2,1,0:T(8,128)}, f32[75,8,128]{2,1,0:T(8,128)}, f32[75,8,128]{2,1,0:T(8,128)}) custom-call(f32[75,8,128]{2,1,0:T(8,128)S(1)} %get-tuple-element.42.refs_0_, f32[75,8,128]{2,1,0:T(8,128)S(1)} %get-tuple-element.43.refs_1_, f32[75,8,128]{2,1,0:T(8,128)S(1)} %get-tuple-element.44.refs_2_, ...), custom_call_target="tpu_custom_call" | custom-call | tf_op jit(solution)/shard_map/pallas_call | solution.py:338
  (4 shorter events, 0.0 us)
Async XLA Ops:
  2.0 21.3 %collective-permute-start = (f32[304,128]{1,0:T(8,128)S(1)}, f32[304,128]{1,0:T(8,128)S(1)}, u32[]{:S(2)}, u32[]{:S(2)}) collective-permute-start(f32[304,128]{1,0:T(8,128)S(1)} %get-tuple-element.49.refs_8_), channel_id=1, source_target_pairs={{0,1},{1,0},{4,5},{5,4},{8,9},{9,8},{12,13},{13,12},{16,17},{17,16... | collective-permute-start | bytes 466952 | tf_op jit(solution)/shard_map/ppermute | solution.py:387
  4.0 34.9 %collective-permute-start.1 = (f32[304,128]{1,0:T(8,128)S(1)}, f32[304,128]{1,0:T(8,128)S(1)}, u32[]{:S(2)}, u32[]{:S(2)}) collective-permute-start(f32[304,128]{1,0:T(8,128)S(1)} %get-tuple-element.49.refs_8_), channel_id=1, source_target_pairs={{2,3},{3,2},{6,7},{7,6},{10,11},{11,10},{14,15},{15,14},{18,19},{1... | collective-permute-start | bytes 466952 | tf_op jit(solution)/shard_map/ppermute | solution.py:387
  4.6 39.9 %collective-permute-start.2 = (f32[304,128]{1,0:T(8,128)S(1)}, f32[304,128]{1,0:T(8,128)S(1)}, u32[]{:S(2)}, u32[]{:S(2)}) collective-permute-start(f32[304,128]{1,0:T(8,128)S(1)} %get-tuple-element.50.refs_9_), channel_id=1, source_target_pairs={{2,1},{3,4},{6,5},{7,8},{10,9},{11,12},{14,13},{15,511},{18,17},{1... | collective-permute-start | bytes 466952 | tf_op jit(solution)/shard_map/ppermute | solution.py:387
  5.9 56.9 %collective-permute-start.3 = (f32[304,128]{1,0:T(8,128)S(1)}, f32[304,128]{1,0:T(8,128)S(1)}, u32[]{:S(2)}, u32[]{:S(2)}) collective-permute-start(f32[304,128]{1,0:T(8,128)S(1)} %get-tuple-element.50.refs_9_), channel_id=1, source_target_pairs={{1,2},{4,3},{5,6},{8,7},{9,10},{12,11},{13,14},{17,18},{20,19},{21... | collective-permute-start | bytes 466952 | tf_op jit(solution)/shard_map/ppermute | solution.py:387
  22.0 20.4 %collective-permute-start.8 = (f32[8,128]{1,0:T(8,128)S(1)}, f32[8,128]{1,0:T(8,128)S(1)}, u32[]{:S(2)}, u32[]{:S(2)}) collective-permute-start(f32[8,128]{1,0:T(8,128)S(1)} %get-tuple-element.55), channel_id=1, source_target_pairs={{498,1},{3,500},{502,5},{7,504},{506,9},{11,508},{510,13},{15,495}... | collective-permute-start | bytes 12296 | tf_op jit(solution)/shard_map/ppermute | solution.py:387
  23.4 20.5 %collective-permute-start.9 = (f32[8,128]{1,0:T(8,128)S(1)}, f32[8,128]{1,0:T(8,128)S(1)}, u32[]{:S(2)}, u32[]{:S(2)}) collective-permute-start(f32[8,128]{1,0:T(8,128)S(1)} %get-tuple-element.55), channel_id=1, source_target_pairs={{1,498},{500,3},{5,502},{504,7},{9,506},{508,11},{13,510},{17,2},{... | collective-permute-start | bytes 12296 | tf_op jit(solution)/shard_map/ppermute | solution.py:387
  38.9 23.9 %collective-permute-start.4 = (f32[40,128]{1,0:T(8,128)S(1)}, f32[40,128]{1,0:T(8,128)S(1)}, u32[]{:S(2)}, u32[]{:S(2)}) collective-permute-start(f32[40,128]{1,0:T(8,128)S(1)} %get-tuple-element.51.refs_6_), channel_id=1, source_target_pairs={{0,16},{16,0},{32,48},{48,32},{64,80},{80,64},{96,112},{112,96},{1... | collective-permute-start | bytes 61448 | tf_op jit(solution)/shard_map/ppermute | solution.py:387
  42.4 15.4 %copy-start = (f32[74,8,128]{2,1,0:T(8,128)S(1)}, f32[74,8,128]{2,1,0:T(8,128)}, u32[]{:S(2)}) copy-start(f32[74,8,128]{2,1,0:T(8,128)} %refs_4_.5) | copy-start | bytes 909316
  42.5 20.4 %collective-permute-start.5 = (f32[40,128]{1,0:T(8,128)S(1)}, f32[40,128]{1,0:T(8,128)S(1)}, u32[]{:S(2)}, u32[]{:S(2)}) collective-permute-start(f32[40,128]{1,0:T(8,128)S(1)} %get-tuple-element.52.refs_7_), channel_id=1, source_target_pairs={{16,32},{32,16},{48,64},{64,48},{80,96},{96,80},{112,128},{128,112... | collective-permute-start | bytes 61448 | tf_op jit(solution)/shard_map/ppermute | solution.py:387
  43.9 19.0 %collective-permute-start.6 = (f32[40,128]{1,0:T(8,128)S(1)}, f32[40,128]{1,0:T(8,128)S(1)}, u32[]{:S(2)}, u32[]{:S(2)}) collective-permute-start(f32[40,128]{1,0:T(8,128)S(1)} %get-tuple-element.53.refs_14_), channel_id=1, source_target_pairs={{2,18},{18,2},{34,50},{50,34},{66,82},{82,66},{98,114},{114,98},{1... | collective-permute-start | bytes 61448 | tf_op jit(solution)/shard_map/ppermute | solution.py:387
  44.6 18.3 %collective-permute-start.7 = (f32[40,128]{1,0:T(8,128)S(1)}, f32[40,128]{1,0:T(8,128)S(1)}, u32[]{:S(2)}, u32[]{:S(2)}) collective-permute-start(f32[40,128]{1,0:T(8,128)S(1)} %get-tuple-element.54.refs_15_), channel_id=1, source_target_pairs={{0,496},{1,497},{18,34},{34,18},{50,66},{66,50},{82,98},{98,82},{1... | collective-permute-start | bytes 61448 | tf_op jit(solution)/shard_map/ppermute | solution.py:387

commit v3 on v2

--- a/solution.py
+++ b/solution.py
@@ -13,6 +13,7 @@
 
 ROWS, LANES = 8, 128
 VMEM_GRANT = 8 << 20
+UNROLL = 5
 COL_ROWS = 40
 
 
@@ -50,7 +51,8 @@
 
 def place_of(n_lat, n_lon):
     lat, lon = lax.axis_index("lat"), lax.axis_index("lon")
-    return lat, lon, lax.rem(lat, 4) < 2, lat == n_lat - 1, lon == n_lon - 1
+    first = lax.rem(lat, 4) < 2
+    return lat, lon, first, jnp.logical_and(first, lon < n_lon // 2), lat == n_lat - 1
 
 
 def pack_rows(mesh_size, levels, t, s, u, v, depth, t_out, s_out, u_out, v_out, h_out, to_a, to_b, corner, ints, sems):
@@ -129,27 +131,28 @@
 def local_work(mesh_size, levels, total, early, *refs):
     t, s, u, v, mix, depth = refs[:6]
     st, ss, su, sv, ra, aa, ba = refs[-7:]
-    lat, _, first, _, _ = place_of(*mesh_size)
-
-    @pl.when(first if early else jnp.logical_not(first))
+    lat, _, _, soon, _ = place_of(*mesh_size)
+
+    @pl.when(soon if early else jnp.logical_not(soon))
     def _():
         lane, row = lane_ids(), row_ids()
         h = depth[...]
         f4 = (0.25 * DT) * coriolis_rows(lat, total)
         open_e = jnp.where(lane < LANES - 1, jnp.minimum(h, roll(h, -1, 1)), 0.0)
         open_n = jnp.where(row < ROWS - 1, jnp.minimum(h, roll(h, -1, 0)), 0.0)
-        zero = jnp.zeros((ROWS, LANES), jnp.float32)
-        one = jnp.ones((ROWS, LANES), jnp.float32)
-        summed, c_here = zero, zero
-        minor, minor_prev = one, zero
-        for k in range(levels):
-            at = slice(k * ROWS, (k + 1) * ROWS)
+        zero = h - h
+        one = zero + 1.0
+
+        def level(k, carry):
+            summed, c_here, minor, minor_prev = carry
+            kf = jnp.asarray(k, jnp.float32)
+            at = pl.ds(pl.multiple_of(k * ROWS, ROWS), ROWS)
             tk, sk, uk, vk = t[at, :], s[at, :], u[at, :], v[at, :]
-            wet = h > float(k)
+            wet = h > kf
             dens = jnp.where(wet, PRESSURE * density_of(tk, sk), 0.0)
             summed = summed + dens
             p = summed - 0.5 * dens
-            me, mn = open_e > float(k), open_n > float(k)
+            me, mn = open_e > kf, open_n > kf
             half_u, half_v = 0.5 * uk, 0.5 * vk
             e0, e1 = jnp.where(me, half_u + 0.5, 0.0), jnp.where(me, half_u - 0.5, 0.0)
             n0, n1 = jnp.where(mn, half_v + 0.5, 0.0), jnp.where(mn, half_v - 0.5, 0.0)
@@ -165,25 +168,26 @@
             u4 = (uk + uw) + (un + roll(uw, -1, 0))
             su[k] = uk + f4 * v4 - DT * (roll(p, -1, 1) - p) + 0.1 * lap_u
             sv[k] = vk - f4 * u4 - DT * (roll(p, -1, 0) - p) + 0.1 * lap_v
-            c_next = jnp.where(h > float(k + 1), DT * mix[k], 0.0) if k < levels - 1 else zero
+            below = mix[jnp.minimum(k, levels - 2)]
+            c_next = jnp.where(h > kf + 1.0, DT * below, 0.0)
             minor_next = (1.0 + c_here + c_next) * minor - (c_here * c_here) * minor_prev
             r = jnp.where(wet, minor / minor_next, 0.0)
-            minor_prev, minor = minor, minor_next
             ra[k] = r
             aa[k] = c_here * r
             ba[k] = c_next * r
-            c_here = c_next
+            return summed, c_next, minor_next, minor
+
+        lax.fori_loop(0, levels, level, (zero, zero, one, zero), unroll=UNROLL)
 
 
 def finish(mesh_size, levels, total, *refs):
     (st, ss, su, sv, ra, aa, ba, depth, to_a, to_b, a_p, a_q, b_p, b_q, c_own, d_own,
      c_p, d_p, c_q, d_q, corner_p, corner_q, ot, os, ou, ov, north, south, kept) = refs
-    lat, lon, first, top, lon_last = place_of(*mesh_size)
+    lat, lon, first, _, top = place_of(*mesh_size)
     lane, row = lane_ids(), row_ids()
     lat_even = lax.rem(lat, 2) == 0
     lon_even = lax.rem(lon, 2) == 0
     b_first = jnp.logical_or(first, top)
-    d_first = jnp.logical_and(first, jnp.logical_not(lon_last))
     h = depth[...]
     f4 = (0.25 * DT) * coriolis_rows(lat, total)
     f7, f0 = f4[7:8, :], f4[0:1, :]
@@ -243,12 +247,21 @@
 
     def tiles(c, d, f):
         at = slice(f * ROWS, (f + 1) * ROWS)
-        x = jnp.where(first, c[0][at, :], c[1][at, :])
-        y = jnp.where(d[2], d[0][at, :], d[1][at, :])
+        x, y = c(at), d(at)
         return jnp.where(lon_even, x, y), jnp.where(lon_even, y, x)
 
-    got_c, got_d = (c_p, c_q), (d_p, d_q, d_first)
-    own_c, own_d = (c_own, c_own), (d_own, d_own, first)
+    def got_c(at):
+        return jnp.where(first, c_p[at, :], c_q[at, :])
+
+    def got_d(at):
+        return jnp.where(first, d_p[at, :], d_q[at, :])
+
+    def own_c(at):
+        return c_own[at, :]
+
+    def own_d(at):
+        return d_own[at, :]
+
     (te, tw), (se, sw), (ue, uw), (ve, vw), (ce, cw) = (tiles(got_c, got_d, f) for f in range(5))
     (t9, tz), (s9, sz), (u9, uz), (v9, vz) = (tiles(own_c, own_d, f) for f in range(4))
     cb = jnp.where(b_first, corner_p[...], corner_q[...])
@@ -284,45 +297,59 @@
     at_n, at_s = row == ROWS - 1, row == 0
     at_e, at_w = lane == LANES - 1, lane == 0
     inner, last = elimination_constants(levels)
-    pt = ps = pu = pv = jnp.zeros((ROWS, LANES), jnp.float32)
-    cs = jnp.zeros((1, LANES), jnp.float32)
-    for k in range(levels):
-
-        def spread(f, de, dw, extra=None):
-            n = north[f, k : k + 1, :]
+    head = levels % UNROLL + UNROLL
+    sides = ((dt_e, dt_w), (ds_e, ds_w), (du_e, du_w), (dv_e, dv_w))
+
+    def down(k, c, carry):
+        pt, ps, pu, pv, cs = carry
+        kf = jnp.asarray(k, jnp.float32)
+        one = pl.ds(k, 1)
+
+        def spread(f, extra=None):
+            n = north[f, one, :]
             if extra is not None:
                 n = n - extra
-            base = jnp.where(at_n, n, jnp.where(at_s, south[f, k : k + 1, :], 0.0))
-            side = jnp.where(at_e, de[:, k : k + 1], jnp.where(at_w, dw[:, k : k + 1], 0.0))
-            return base + side
-
-        dn = north[4, k : k + 1, :]
+            base = jnp.where(at_n, n, jnp.where(at_s, south[f, one, :], 0.0))
+            de = pltpu.roll(sides[f][0], LANES - 1 - k, 1)
+            dw = pltpu.roll(sides[f][1], lax.rem(LANES - k, LANES), 1)
+            return base + jnp.where(at_e, de, jnp.where(at_w, dw, 0.0))
+
+        dn = north[4, one, :]
         cs = cs + dn
         r, a = ra[k], aa[k]
-        pt = r * (st[k] + spread(0, dt_e, dt_w)) + a * pt
-        ps = r * (ss[k] + spread(1, ds_e, ds_w)) + a * ps
-        ru = jnp.where(m_u > float(k + 1), inner[k], jnp.where(m_u > float(k), last[k], 0.0))
-        rv = jnp.where(m_v > float(k + 1), inner[k], jnp.where(m_v > float(k), last[k], 0.0))
-        pu = ru * (su[k] + spread(2, du_e, du_w)) + (VISC_STEP * ru) * pu
-        pv = rv * (sv[k] + spread(3, dv_e, dv_w, cs - 0.5 * dn)) + (VISC_STEP * rv) * pv
-        kept[0, k] = pt
-        kept[1, k] = ps
-        kept[2, k] = pu
-        kept[3, k] = pv
-    xt, xs, xu, xv = pt, ps, pu, pv
-    for k in range(levels - 1, -1, -1):
-        if k < levels - 1:
-            b = ba[k]
-            bu = jnp.where(m_u > float(k + 1), VISC_STEP * inner[k], 0.0)
-            bv = jnp.where(m_v > float(k + 1), VISC_STEP * inner[k], 0.0)
-            xt = kept[0, k] + b * xt
-            xs = kept[1, k] + b * xs
-            xu = kept[2, k] + bu * xu
-            xv = kept[3, k] + bv * xv
-        ot[k] = xt
-        os[k] = xs
-        ou[k] = xu
-        ov[k] = xv
+        ru = jnp.where(m_u > kf + 1.0, inner[c], jnp.where(m_u > kf, last[c], 0.0))
+        rv = jnp.where(m_v > kf + 1.0, inner[c], jnp.where(m_v > kf, last[c], 0.0))
+        pt = r * (st[k] + spread(0)) + a * pt
+        ps = r * (ss[k] + spread(1)) + a * ps
+        pu = ru * (su[k] + spread(2)) + (VISC_STEP * ru) * pu
+        pv = rv * (sv[k] + spread(3, cs - 0.5 * dn)) + (VISC_STEP * rv) * pv
+        for f, x in enumerate((pt, ps, pu, pv)):
+            kept[f, k] = x
+        return pt, ps, pu, pv, cs
+
+    def up(k, c, carry):
+        xt, xs, xu, xv = carry
+        kf = jnp.asarray(k, jnp.float32)
+        b = ba[k]
+        bu = jnp.where(m_u > kf + 1.0, VISC_STEP * inner[c], 0.0)
+        bv = jnp.where(m_v > kf + 1.0, VISC_STEP * inner[c], 0.0)
+        xt = kept[0, k] + b * xt
+        xs = kept[1, k] + b * xs
+        xu = kept[2, k] + bu * xu
+        xv = kept[3, k] + bv * xv
+        ot[k], os[k], ou[k], ov[k] = xt, xs, xu, xv
+        return xt, xs, xu, xv
+
+    zero = h - h
+    carry = (zero, zero, zero, zero, zero[0:1, :])
+    for k in range(head):
+        carry = down(k, k, carry)
+    carry = lax.fori_loop(head, levels, lambda k, x: down(k, head, x), carry, unroll=UNROLL)
+    carry = lax.fori_loop(
+        head, levels, lambda i, x: up(levels - 1 + head - i, head, x), (zero,) * 4, unroll=UNROLL
+    )
+    for k in range(head - 1, -1, -1):
+        carry = up(k, k, carry)
 
 
 HBM = pl.BlockSpec(memory_space=pltpu.HBM)
@@ -368,9 +395,7 @@
         side = "p" if lat % 4 < 2 else "q"
         for lon in range(0, n_lon, 2):
             p["c_" + side] += both(at(lat, lon), at(lat, lon + 1))
-            p["d_" + side].append((at(lat, lon + 1), at(lat, lon + 2)))
-            wraps = lon + 2 == n_lon
-            p["d_q" if wraps else "d_" + side].append((at(lat, lon + 2), at(lat, lon + 1)))
+            p["d_" + side] += both(at(lat, lon + 1), at(lat, lon + 2))
     return p
 
 

time: 65.9 us -> 63 us (0.956)
  Pallas kernels: 9.81 us -> 8.25 us
  starting transfers between devices: 54.9 us -> 53.6 us
    pallas_call x6, Pallas kernels: 9.81 us -> 8.25 us  [call(): pl.pallas_call(body, out_shape=shapes, in_specs=[HBM] * len(far) + [VMEM]...]
    ppermute x10, starting transfers between devices: 54.9 us -> 53.6 us  [send(): return lax.ppermute(x, ('lon', 'lat'), pairs[name])]
  transfers between devices with their start and end apart: 10 -> 10, of which waited for: 0 -> 0; matrix products, arithmetic and copies ran while one was open for 0% -> 0% of each run, Pallas kernels for 9% -> 5%
where the time goes in v3:
time: 63 us; the launch traced here: 62.7 us
  starting transfers between devices  53.6 us (85%)
  Pallas kernels  8.25 us (13%)
  between operations  0.84 us (1%)
    ppermute x10, starting transfers between devices, send(): return lax.ppermute(x, ('lon', 'lat'), pairs[name])  53.6 us
    pallas_call x6, Pallas kernels, call(): pl.pallas_call(body, out_shape=shapes, in_specs=[HBM] * len(far) + [VMEM]...  8.25 us
  transfers between devices with their start and end apart: 10, of which 0 were waited for; matrix products, arithmetic and copies ran while one was open for 0% of the time, Pallas kernels for 5%

profile of v3, /device:TPU:6, one launch (start us, length us, event | category | flops | bytes accessed | tf_op | source)
XLA Modules:
  0.0 62.7 jit_solution(8645961755885253867)
XLA Ops:
  0.6 1.4 %shard_map.93 = (f32[600,128]{1,0:T(8,128)S(1)}, f32[600,128]{1,0:T(8,128)S(1)}, f32[600,128]{1,0:T(8,128)S(1)}, f32[600,128]{1,0:T(8,128)S(1)}, f32[8,128]{1,0:...) custom-call(f32[600,128]{1,0:T(8,128)} %bitcast.4, f32[600,128]{1,0:T(8,128)} %bitcast.5, ...), custom_call_target="tpu_custom_call" | custom-call | tf_op jit(solution)/shard_map/pallas_call | solution.py:365
  2.0 1.9 %collective-permute-start = (f32[304,128]{1,0:T(8,128)S(1)}, f32[304,128]{1,0:T(8,128)S(1)}, u32[]{:S(2)}, u32[]{:S(2)}) collective-permute-start(f32[304,128]{1,0:T(8,128)S(1)} %get-tuple-element.49.refs_8_), channel_id=1, source_target_pairs={{0,1},{1,0},{4,5},{5,4},{8,9},{9,8},{12,13},{13,12},{16,17},{17,16... | collective-permute-start | bytes 466952 | tf_op jit(solution)/shard_map/ppermute | solution.py:412
  4.0 0.7 %collective-permute-start.1 = (f32[304,128]{1,0:T(8,128)S(1)}, f32[304,128]{1,0:T(8,128)S(1)}, u32[]{:S(2)}, u32[]{:S(2)}) collective-permute-start(f32[304,128]{1,0:T(8,128)S(1)} %get-tuple-element.49.refs_8_), channel_id=1, source_target_pairs={{2,3},{3,2},{6,7},{7,6},{10,11},{11,10},{14,15},{15,14},{18,19},{1... | collective-permute-start | bytes 466952 | tf_op jit(solution)/shard_map/ppermute | solution.py:412
  4.6 1.3 %collective-permute-start.2 = (f32[304,128]{1,0:T(8,128)S(1)}, f32[304,128]{1,0:T(8,128)S(1)}, u32[]{:S(2)}, u32[]{:S(2)}) collective-permute-start(f32[304,128]{1,0:T(8,128)S(1)} %get-tuple-element.50.refs_9_), channel_id=1, source_target_pairs={{2,1},{3,4},{6,5},{7,8},{10,9},{11,12},{14,13},{15,511},{18,17},{1... | collective-permute-start | bytes 466952 | tf_op jit(solution)/shard_map/ppermute | solution.py:412
  5.9 16.1 %collective-permute-start.3 = (f32[304,128]{1,0:T(8,128)S(1)}, f32[304,128]{1,0:T(8,128)S(1)}, u32[]{:S(2)}, u32[]{:S(2)}) collective-permute-start(f32[304,128]{1,0:T(8,128)S(1)} %get-tuple-element.50.refs_9_), channel_id=1, source_target_pairs={{1,2},{4,3},{5,6},{8,7},{9,10},{12,11},{13,14},{17,18},{20,19},{21... | collective-permute-start | bytes 466952 | tf_op jit(solution)/shard_map/ppermute | solution.py:412
  22.0 1.3 %collective-permute-start.8 = (f32[8,128]{1,0:T(8,128)S(1)}, f32[8,128]{1,0:T(8,128)S(1)}, u32[]{:S(2)}, u32[]{:S(2)}) collective-permute-start(f32[8,128]{1,0:T(8,128)S(1)} %get-tuple-element.55), channel_id=1, source_target_pairs={{498,1},{3,500},{502,5},{7,504},{506,9},{11,508},{510,13},{15,495}... | collective-permute-start | bytes 12296 | tf_op jit(solution)/shard_map/ppermute | solution.py:412
  23.3 0.0 collective-permute-done.refs_5_.refs_10_
  23.4 14.8 %collective-permute-start.9 = (f32[8,128]{1,0:T(8,128)S(1)}, f32[8,128]{1,0:T(8,128)S(1)}, u32[]{:S(2)}, u32[]{:S(2)}) collective-permute-start(f32[8,128]{1,0:T(8,128)S(1)} %get-tuple-element.55), channel_id=1, source_target_pairs={{1,498},{500,3},{5,502},{504,7},{9,506},{508,11},{13,510},{17,2},{... | collective-permute-start | bytes 12296 | tf_op jit(solution)/shard_map/ppermute | solution.py:412
  38.1 0.7 %shard_map.96 = (f32[40,128]{1,0:T(8,128)S(1)}, f32[40,128]{1,0:T(8,128)S(1)}) custom-call(f32[600,128]{1,0:T(8,128)S(1)} %get-tuple-element.30.refs_0_, f32[600,128]{1,0:T(8,128)S(1)} %get-tuple-element.31.refs_1_, f32[600,128]{1,0:T(8,128)S(1)} %get-tuple-element.32.refs_2_, f32[600,128]{1,0:T(8,128)S(1)} %get-tuple-element.33.refs_3_, ...), custom_call_target="tpu_custom_call" | custom-call | tf_op jit(solution)/shard_map/pallas_call | solution.py:365
  38.9 0.0 collective-permute-done.1.refs_5_.refs_11_
  38.9 3.5 %collective-permute-start.4 = (f32[40,128]{1,0:T(8,128)S(1)}, f32[40,128]{1,0:T(8,128)S(1)}, u32[]{:S(2)}, u32[]{:S(2)}) collective-permute-start(f32[40,128]{1,0:T(8,128)S(1)} %get-tuple-element.51.refs_6_), channel_id=1, source_target_pairs={{0,16},{16,0},{32,48},{48,32},{64,80},{80,64},{96,112},{112,96},{1... | collective-permute-start | bytes 61448 | tf_op jit(solution)/shard_map/ppermute | solution.py:412
  42.4 0.0 copy-start
  42.4 0.0 collective-permute-done.8.refs_20_
  42.5 12.7 %collective-permute-start.5 = (f32[40,128]{1,0:T(8,128)S(1)}, f32[40,128]{1,0:T(8,128)S(1)}, u32[]{:S(2)}, u32[]{:S(2)}) collective-permute-start(f32[40,128]{1,0:T(8,128)S(1)} %get-tuple-element.52.refs_7_), channel_id=1, source_target_pairs={{16,32},{32,16},{48,64},{64,48},{80,96},{96,80},{112,128},{128,112... | collective-permute-start | bytes 61448 | tf_op jit(solution)/shard_map/ppermute | solution.py:412
  55.2 0.0 collective-permute-done.9.refs_21_
  55.2 0.7 %collective-permute-start.6 = (f32[40,128]{1,0:T(8,128)S(1)}, f32[40,128]{1,0:T(8,128)S(1)}, u32[]{:S(2)}, u32[]{:S(2)}) collective-permute-start(f32[40,128]{1,0:T(8,128)S(1)} %get-tuple-element.53.refs_14_), channel_id=1, source_target_pairs={{2,18},{18,2},{34,50},{50,34},{66,82},{82,66},{98,114},{114,98},{1... | collective-permute-start | bytes 61448 | tf_op jit(solution)/shard_map/ppermute | solution.py:412
  55.8 0.0 collective-permute-done.2.refs_12_
  55.8 0.7 %collective-permute-start.7 = (f32[40,128]{1,0:T(8,128)S(1)}, f32[40,128]{1,0:T(8,128)S(1)}, u32[]{:S(2)}, u32[]{:S(2)}) collective-permute-start(f32[40,128]{1,0:T(8,128)S(1)} %get-tuple-element.54.refs_15_), channel_id=1, source_target_pairs={{18,34},{34,18},{50,66},{66,50},{82,98},{98,82},{114,130},{130,114... | collective-permute-start | bytes 61448 | tf_op jit(solution)/shard_map/ppermute | solution.py:412
  56.5 2.4 %shard_map.94 = (f32[75,8,128]{2,1,0:T(8,128)S(1)}, f32[75,8,128]{2,1,0:T(8,128)S(1)}, f32[75,8,128]{2,1,0:T(8,128)S(1)}, f32[75,8,128]{2,1,0:T(8,128)S(1)}, f32...) custom-call(f32[600,128]{1,0:T(8,128)S(1)} %get-tuple-element.30.refs_0_, ...), custom_call_target="tpu_custom_call" | custom-call | tf_op jit(solution)/shard_map/pallas_call | solution.py:365
  59.0 0.0 collective-permute-done.3.refs_13_
  59.0 0.0 collective-permute-done.4.refs_16_
  59.0 0.0 collective-permute-done.5.refs_17_
  59.0 0.0 collective-permute-done.6.refs_18_
  59.1 3.6 %shard_map.98 = (f32[75,8,128]{2,1,0:T(8,128)}, f32[75,8,128]{2,1,0:T(8,128)}, f32[75,8,128]{2,1,0:T(8,128)}, f32[75,8,128]{2,1,0:T(8,128)}) custom-call(f32[75,8,128]{2,1,0:T(8,128)S(1)} %get-tuple-element.42.refs_0_, f32[75,8,128]{2,1,0:T(8,128)S(1)} %get-tuple-element.43.refs_1_, f32[75,8,128]{2,1,0:T(8,128)S(1)} %get-tuple-element.44.refs_2_, ...), custom_call_target="tpu_custom_call" | custom-call | tf_op jit(solution)/shard_map/pallas_call | solution.py:365
  (4 shorter events, 0.1 us)
Async XLA Ops:
  2.0 21.3 %collective-permute-start = (f32[304,128]{1,0:T(8,128)S(1)}, f32[304,128]{1,0:T(8,128)S(1)}, u32[]{:S(2)}, u32[]{:S(2)}) collective-permute-start(f32[304,128]{1,0:T(8,128)S(1)} %get-tuple-element.49.refs_8_), channel_id=1, source_target_pairs={{0,1},{1,0},{4,5},{5,4},{8,9},{9,8},{12,13},{13,12},{16,17},{17,16... | collective-permute-start | bytes 466952 | tf_op jit(solution)/shard_map/ppermute | solution.py:412
  4.0 34.9 %collective-permute-start.1 = (f32[304,128]{1,0:T(8,128)S(1)}, f32[304,128]{1,0:T(8,128)S(1)}, u32[]{:S(2)}, u32[]{:S(2)}) collective-permute-start(f32[304,128]{1,0:T(8,128)S(1)} %get-tuple-element.49.refs_8_), channel_id=1, source_target_pairs={{2,3},{3,2},{6,7},{7,6},{10,11},{11,10},{14,15},{15,14},{18,19},{1... | collective-permute-start | bytes 466952 | tf_op jit(solution)/shard_map/ppermute | solution.py:412
  4.6 51.2 %collective-permute-start.2 = (f32[304,128]{1,0:T(8,128)S(1)}, f32[304,128]{1,0:T(8,128)S(1)}, u32[]{:S(2)}, u32[]{:S(2)}) collective-permute-start(f32[304,128]{1,0:T(8,128)S(1)} %get-tuple-element.50.refs_9_), channel_id=1, source_target_pairs={{2,1},{3,4},{6,5},{7,8},{10,9},{11,12},{14,13},{15,511},{18,17},{1... | collective-permute-start | bytes 466952 | tf_op jit(solution)/shard_map/ppermute | solution.py:412
  5.9 53.1 %collective-permute-start.3 = (f32[304,128]{1,0:T(8,128)S(1)}, f32[304,128]{1,0:T(8,128)S(1)}, u32[]{:S(2)}, u32[]{:S(2)}) collective-permute-start(f32[304,128]{1,0:T(8,128)S(1)} %get-tuple-element.50.refs_9_), channel_id=1, source_target_pairs={{1,2},{4,3},{5,6},{8,7},{9,10},{12,11},{13,14},{17,18},{20,19},{21... | collective-permute-start | bytes 466952 | tf_op jit(solution)/shard_map/ppermute | solution.py:412
  22.0 20.4 %collective-permute-start.8 = (f32[8,128]{1,0:T(8,128)S(1)}, f32[8,128]{1,0:T(8,128)S(1)}, u32[]{:S(2)}, u32[]{:S(2)}) collective-permute-start(f32[8,128]{1,0:T(8,128)S(1)} %get-tuple-element.55), channel_id=1, source_target_pairs={{498,1},{3,500},{502,5},{7,504},{506,9},{11,508},{510,13},{15,495}... | collective-permute-start | bytes 12296 | tf_op jit(solution)/shard_map/ppermute | solution.py:412
  23.4 31.8 %collective-permute-start.9 = (f32[8,128]{1,0:T(8,128)S(1)}, f32[8,128]{1,0:T(8,128)S(1)}, u32[]{:S(2)}, u32[]{:S(2)}) collective-permute-start(f32[8,128]{1,0:T(8,128)S(1)} %get-tuple-element.55), channel_id=1, source_target_pairs={{1,498},{500,3},{5,502},{504,7},{9,506},{508,11},{13,510},{17,2},{... | collective-permute-start | bytes 12296 | tf_op jit(solution)/shard_map/ppermute | solution.py:412
  38.9 20.1 %collective-permute-start.4 = (f32[40,128]{1,0:T(8,128)S(1)}, f32[40,128]{1,0:T(8,128)S(1)}, u32[]{:S(2)}, u32[]{:S(2)}) collective-permute-start(f32[40,128]{1,0:T(8,128)S(1)} %get-tuple-element.51.refs_6_), channel_id=1, source_target_pairs={{0,16},{16,0},{32,48},{48,32},{64,80},{80,64},{96,112},{112,96},{1... | collective-permute-start | bytes 61448 | tf_op jit(solution)/shard_map/ppermute | solution.py:412
  42.4 14.1 %copy-start = (f32[74,8,128]{2,1,0:T(8,128)S(1)}, f32[74,8,128]{2,1,0:T(8,128)}, u32[]{:S(2)}) copy-start(f32[74,8,128]{2,1,0:T(8,128)} %refs_4_.5) | copy-start | bytes 909316
  42.5 16.6 %collective-permute-start.5 = (f32[40,128]{1,0:T(8,128)S(1)}, f32[40,128]{1,0:T(8,128)S(1)}, u32[]{:S(2)}, u32[]{:S(2)}) collective-permute-start(f32[40,128]{1,0:T(8,128)S(1)} %get-tuple-element.52.refs_7_), channel_id=1, source_target_pairs={{16,32},{32,16},{48,64},{64,48},{80,96},{96,80},{112,128},{128,112... | collective-permute-start | bytes 61448 | tf_op jit(solution)/shard_map/ppermute | solution.py:412
  55.2 3.9 %collective-permute-start.6 = (f32[40,128]{1,0:T(8,128)S(1)}, f32[40,128]{1,0:T(8,128)S(1)}, u32[]{:S(2)}, u32[]{:S(2)}) collective-permute-start(f32[40,128]{1,0:T(8,128)S(1)} %get-tuple-element.53.refs_14_), channel_id=1, source_target_pairs={{2,18},{18,2},{34,50},{50,34},{66,82},{82,66},{98,114},{114,98},{1... | collective-permute-start | bytes 61448 | tf_op jit(solution)/shard_map/ppermute | solution.py:412
  55.8 3.2 %collective-permute-start.7 = (f32[40,128]{1,0:T(8,128)S(1)}, f32[40,128]{1,0:T(8,128)S(1)}, u32[]{:S(2)}, u32[]{:S(2)}) collective-permute-start(f32[40,128]{1,0:T(8,128)S(1)} %get-tuple-element.54.refs_15_), channel_id=1, source_target_pairs={{18,34},{34,18},{50,66},{66,50},{82,98},{98,82},{114,130},{130,114... | collective-permute-start | bytes 61448 | tf_op jit(solution)/shard_map/ppermute | solution.py:412

commit v4 on v3

--- a/solution.py
+++ b/solution.py
@@ -108,8 +108,8 @@
             west = jnp.zeros((ROWS, LANES), jnp.float32)
             for k in range(levels):
                 x = ref[k * ROWS : (k + 1) * ROWS, :]
-                east = jnp.where(lane == k, x[:, LANES - 1 : LANES], east)
-                west = jnp.where(lane == k, x[:, 0:1], west)
+                east = jnp.where(lane == k, roll(x, k + 1, 1), east)
+                west = jnp.where(lane == k, roll(x, k, 1), west)
             if f == 0:
                 east = jnp.where(lane == levels, h[:, LANES - 1 : LANES], east)
                 west = jnp.where(lane == levels, h[:, 0:1], west)
@@ -121,6 +121,19 @@
         west = jnp.broadcast_to(jnp.where(lat_even, 0.0, cv), (ROWS, LANES))
         to_c[4 * ROWS : 5 * ROWS, :] = jnp.where(lon_even, east, west)
         to_d[4 * ROWS : 5 * ROWS, :] = jnp.where(lon_even, west, east)
+
+
+def pack_far(mesh_size, levels, to_b, from_c, from_d, out):
+    lat, lon, first, _, _ = place_of(*mesh_size)
+    lon_even = lax.rem(lon, 2) == 0
+
+    @pl.when(first)
+    def _():
+        out[...] = to_b[...]
+        v_east = jnp.where(lon_even, from_c[4 * ROWS - 1 : 4 * ROWS, :], from_d[4 * ROWS - 1 : 4 * ROWS, :])
+        u_west = jnp.where(lon_even, from_d[2 * ROWS : 2 * ROWS + 1, :], from_c[2 * ROWS : 2 * ROWS + 1, :])
+        at = 4 * levels + 1
+        out[at : at + 1, :] = jnp.where(lax.rem(lat, 2) == 0, u_west, v_east)
 
 
 def coriolis_rows(lat, total):
@@ -182,7 +195,7 @@
 
 def finish(mesh_size, levels, total, *refs):
     (st, ss, su, sv, ra, aa, ba, depth, to_a, to_b, a_p, a_q, b_p, b_q, c_own, d_own,
-     c_p, d_p, c_q, d_q, corner_p, corner_q, ot, os, ou, ov, north, south, kept) = refs
+     c_p, d_p, c_q, d_q, corner, ot, os, ou, ov, north, south, kept) = refs
     lat, lon, first, _, top = place_of(*mesh_size)
     lane, row = lane_ids(), row_ids()
     lat_even = lax.rem(lat, 2) == 0
@@ -264,9 +277,9 @@
 
     (te, tw), (se, sw), (ue, uw), (ve, vw), (ce, cw) = (tiles(got_c, got_d, f) for f in range(5))
     (t9, tz), (s9, sz), (u9, uz), (v9, vz) = (tiles(own_c, own_d, f) for f in range(4))
-    cb = jnp.where(b_first, corner_p[...], corner_q[...])
-    cb_u = jnp.broadcast_to(cb[0:1, :], (ROWS, LANES))
-    cb_v = jnp.broadcast_to(cb[1:2, :], (ROWS, LANES))
+    late = b_q[4 * levels + 1 : 4 * levels + 2, :]
+    cb_u = jnp.broadcast_to(jnp.where(b_first, corner[0:1, :], late), (ROWS, LANES))
+    cb_v = jnp.broadcast_to(jnp.where(b_first, corner[1:2, :], late), (ROWS, LANES))
     south_east = jnp.where(lat_even, cb_v, ce)
     north_west = jnp.where(lat_even, cw, jnp.where(top, 0.0, cb_u))
     north_end = jnp.where(jnp.logical_and(top, row == ROWS - 1), -cb_u, 0.0)
@@ -297,7 +310,6 @@
     at_n, at_s = row == ROWS - 1, row == 0
     at_e, at_w = lane == LANES - 1, lane == 0
     inner, last = elimination_constants(levels)
-    head = levels % UNROLL + UNROLL
     sides = ((dt_e, dt_w), (ds_e, ds_w), (du_e, du_w), (dv_e, dv_w))
 
     def down(k, c, carry):
@@ -311,7 +323,7 @@
                 n = n - extra
             base = jnp.where(at_n, n, jnp.where(at_s, south[f, one, :], 0.0))
             de = pltpu.roll(sides[f][0], LANES - 1 - k, 1)
-            dw = pltpu.roll(sides[f][1], lax.rem(LANES - k, LANES), 1)
+            dw = pltpu.roll(sides[f][1], (LANES - k) % LANES, 1)
             return base + jnp.where(at_e, de, jnp.where(at_w, dw, 0.0))
 
         dn = north[4, one, :]
@@ -342,13 +354,10 @@
 
     zero = h - h
     carry = (zero, zero, zero, zero, zero[0:1, :])
-    for k in range(head):
+    for k in range(levels):
         carry = down(k, k, carry)
-    carry = lax.fori_loop(head, levels, lambda k, x: down(k, head, x), carry, unroll=UNROLL)
-    carry = lax.fori_loop(
-        head, levels, lambda i, x: up(levels - 1 + head - i, head, x), (zero,) * 4, unroll=UNROLL
-    )
-    for k in range(head - 1, -1, -1):
+    carry = (zero,) * 4
+    for k in range(levels - 1, -1, -1):
         carry = up(k, k, carry)
 
 
@@ -388,7 +397,8 @@
             for x, y in both((lat, lon), (lat + 1, lon)):
                 p["b_p" if y[0] % 4 < 2 else "b_q"].append((at(*x), at(*y)))
             for x, y in both((lat, lon), (lat + 1, lon - 1)):
-                p["k_p" if y[0] % 4 < 2 else "k_q"].append((at(*x), at(*y)))
+                if y[0] % 4 < 2:
+                    p["k_p"].append((at(*x), at(*y)))
         p["b_p"].append((at(n_lat - 1, lon), at(n_lat - 1, n_lon - 1 - lon)))
         p["k_p"].append((at(n_lat - 1, lon), at(n_lat - 1, n_lon - 2 - lon)))
     for lat in range(n_lat):
@@ -426,8 +436,8 @@
     d_p = send(cols_p[1], "d_p")
     c_p = send(cols_p[0], "c_p")
     work = call(bind(local_work, total, True), [], [*fields, mix, depth], [full] * 7)
-    b_q = send(to_b, "b_q")
-    k_q = send(to_corner, "k_q")
+    (to_far,) = call(bind(pack_far), [], [to_b, c_p, d_p], [rows])
+    b_q = send(to_far, "b_q")
     a_q = send(to_a, "a_q")
     cols_q = call(bind(pack_columns, False), [], [*fields, depth, a_q, *cols_p], [column] * 2)
     d_q = send(cols_q[1], "d_q")
@@ -440,7 +450,7 @@
     return tuple(
         call(
             bind(finish, total), [],
-            [*work, depth, to_a, to_b, a_p, a_q, b_p, b_q, *cols_q, c_p, d_p, c_q, d_q, k_p, k_q],
+            [*work, depth, to_a, to_b, a_p, a_q, b_p, b_q, *cols_q, c_p, d_p, c_q, d_q, k_p],
             [full] * 4,
             [
                 pltpu.VMEM((5, padded, LANES), jnp.float32),

time: 63 us -> 59.2 us (0.940)
  starting transfers between devices: 53.6 us -> 38.4 us
  waiting for transfers between devices: 0.03 us -> 12.8 us
  Pallas kernels: 8.25 us -> 7.02 us
    ppermute x10 -> x9, starting transfers between devices: 53.6 us -> 38.4 us  [send(): return lax.ppermute(x, ('lon', 'lat'), pairs[name])]
    ppermute x10 -> x9, waiting for transfers between devices: 0.03 us -> 12.8 us  [send(): return lax.ppermute(x, ('lon', 'lat'), pairs[name])]
    pallas_call x6 -> x7, Pallas kernels: 8.25 us -> 7.02 us  [call(): pl.pallas_call(body, out_shape=shapes, in_specs=[HBM] * len(far) + [VMEM]...]
  transfers between devices with their start and end apart: 10 -> 9, of which waited for: 0 -> 3; matrix products, arithmetic and copies ran while one was open for 0% -> 0% of each run, Pallas kernels for 5% -> 5%
where the time goes in v4:
time: 59.2 us; the launch traced here: 59 us
  starting transfers between devices  38.4 us (65%)
  waiting for transfers between devices  12.8 us (22%)
  Pallas kernels  7.02 us (12%)
  between operations  0.79 us (1%)
    ppermute x9, starting transfers between devices, send(): return lax.ppermute(x, ('lon', 'lat'), pairs[name])  38.4 us
    ppermute x9, waiting for transfers between devices, send(): return lax.ppermute(x, ('lon', 'lat'), pairs[name])  12.8 us
    pallas_call x7, Pallas kernels, call(): pl.pallas_call(body, out_shape=shapes, in_specs=[HBM] * len(far) + [VMEM]...  7.02 us
  transfers between devices with their start and end apart: 9, of which 3 were waited for; matrix products, arithmetic and copies ran while one was open for 0% of the time, Pallas kernels for 5%

profile of v4, /device:TPU:6, one launch (start us, length us, event | category | flops | bytes accessed | tf_op | source)
XLA Modules:
  0.0 59.0 jit_solution(1897843250304060123)
XLA Ops:
  0.6 1.4 %shard_map.93 = (f32[600,128]{1,0:T(8,128)S(1)}, f32[600,128]{1,0:T(8,128)S(1)}, f32[600,128]{1,0:T(8,128)S(1)}, f32[600,128]{1,0:T(8,128)S(1)}, f32[8,128]{1,0:...) custom-call(f32[600,128]{1,0:T(8,128)} %bitcast.4, f32[600,128]{1,0:T(8,128)} %bitcast.5, ...), custom_call_target="tpu_custom_call" | custom-call | tf_op jit(solution)/shard_map/pallas_call | solution.py:374
  2.0 1.9 %collective-permute-start = (f32[304,128]{1,0:T(8,128)S(1)}, f32[304,128]{1,0:T(8,128)S(1)}, u32[]{:S(2)}, u32[]{:S(2)}) collective-permute-start(f32[304,128]{1,0:T(8,128)S(1)} %get-tuple-element.49.refs_8_), channel_id=1, source_target_pairs={{0,1},{1,0},{4,5},{5,4},{8,9},{9,8},{12,13},{13,12},{16,17},{17,16... | collective-permute-start | bytes 466952 | tf_op jit(solution)/shard_map/ppermute | solution.py:422
  4.0 0.7 %collective-permute-start.1 = (f32[304,128]{1,0:T(8,128)S(1)}, f32[304,128]{1,0:T(8,128)S(1)}, u32[]{:S(2)}, u32[]{:S(2)}) collective-permute-start(f32[304,128]{1,0:T(8,128)S(1)} %get-tuple-element.49.refs_8_), channel_id=1, source_target_pairs={{2,3},{3,2},{6,7},{7,6},{10,11},{11,10},{14,15},{15,14},{18,19},{1... | collective-permute-start | bytes 466952 | tf_op jit(solution)/shard_map/ppermute | solution.py:422
  4.6 0.7 %collective-permute-done.refs_5_.refs_10_ = f32[304,128]{1,0:T(8,128)S(1)} collective-permute-done((f32[304,128]{1,0:T(8,128)S(1)}, f32[304,128]{1,0:T(8,128)S(1)}, u32[]{:S(2)}, u32[]{:S(2)}) %collective-permute-start) | collective-permute-done | bytes 155680 | tf_op jit(solution)/shard_map/ppermute | solution.py:422
  5.3 0.7 %shard_map.96 = (f32[40,128]{1,0:T(8,128)S(1)}, f32[40,128]{1,0:T(8,128)S(1)}) custom-call(f32[600,128]{1,0:T(8,128)S(1)} %get-tuple-element.30.refs_0_, f32[600,128]{1,0:T(8,128)S(1)} %get-tuple-element.31.refs_1_, f32[600,128]{1,0:T(8,128)S(1)} %get-tuple-element.32.refs_2_, f32[600,128]{1,0:T(8,128)S(1)} %get-tuple-element.33.refs_3_, ...), custom_call_target="tpu_custom_call" | custom-call | tf_op jit(solution)/shard_map/pallas_call | solution.py:374
  6.0 3.5 %collective-permute-start.3 = (f32[40,128]{1,0:T(8,128)S(1)}, f32[40,128]{1,0:T(8,128)S(1)}, u32[]{:S(2)}, u32[]{:S(2)}) collective-permute-start(f32[40,128]{1,0:T(8,128)S(1)} %get-tuple-element.51.refs_6_), channel_id=1, source_target_pairs={{0,16},{16,0},{32,48},{48,32},{64,80},{80,64},{96,112},{112,96},{1... | collective-permute-start | bytes 61448 | tf_op jit(solution)/shard_map/ppermute | solution.py:422
  9.5 14.8 %collective-permute-start.4 = (f32[40,128]{1,0:T(8,128)S(1)}, f32[40,128]{1,0:T(8,128)S(1)}, u32[]{:S(2)}, u32[]{:S(2)}) collective-permute-start(f32[40,128]{1,0:T(8,128)S(1)} %get-tuple-element.52.refs_7_), channel_id=1, source_target_pairs={{16,32},{32,16},{48,64},{64,48},{80,96},{96,80},{112,128},{128,112... | collective-permute-start | bytes 61448 | tf_op jit(solution)/shard_map/ppermute | solution.py:422
  24.3 1.3 %collective-permute-start.2 = (f32[304,128]{1,0:T(8,128)S(1)}, f32[304,128]{1,0:T(8,128)S(1)}, u32[]{:S(2)}, u32[]{:S(2)}) collective-permute-start(f32[304,128]{1,0:T(8,128)S(1)} %get-tuple-element.50.refs_0_.refs_9_), channel_id=1, source_target_pairs={{2,1},{3,4},{6,5},{7,8},{10,9},{11,12},{14,13},{15,511},{18,17},{1... | collective-permute-start | bytes 466952 | tf_op jit(solution)/shard_map/ppermute | solution.py:422
  25.6 0.0 collective-permute-done.3.refs_1_.refs_16_
  25.6 0.4 collective-permute-done.4.refs_2_.refs_17_
  26.1 0.0 copy-start
  26.1 13.6 %collective-permute-start.5 = (f32[304,128]{1,0:T(8,128)S(1)}, f32[304,128]{1,0:T(8,128)S(1)}, u32[]{:S(2)}, u32[]{:S(2)}) collective-permute-start(f32[304,128]{1,0:T(8,128)S(1)} %shard_map.97), channel_id=1, source_target_pairs={{1,2},{4,3},{5,6},{8,7},{9,10},{12,11},{13,14},{17,18},{20,19},{21... | collective-permute-start | bytes 466952 | tf_op jit(solution)/shard_map/ppermute | solution.py:422
  39.7 0.0 collective-permute-done.1.refs_5_.refs_11_
  39.8 0.7 %collective-permute-start.6 = (f32[40,128]{1,0:T(8,128)S(1)}, f32[40,128]{1,0:T(8,128)S(1)}, u32[]{:S(2)}, u32[]{:S(2)}) collective-permute-start(f32[40,128]{1,0:T(8,128)S(1)} %get-tuple-element.53.refs_14_), channel_id=1, source_target_pairs={{2,18},{18,2},{34,50},{50,34},{66,82},{82,66},{98,114},{114,98},{1... | collective-permute-start | bytes 61448 | tf_op jit(solution)/shard_map/ppermute | solution.py:422
  40.4 0.7 %collective-permute-start.7 = (f32[40,128]{1,0:T(8,128)S(1)}, f32[40,128]{1,0:T(8,128)S(1)}, u32[]{:S(2)}, u32[]{:S(2)}) collective-permute-start(f32[40,128]{1,0:T(8,128)S(1)} %get-tuple-element.54.refs_15_), channel_id=1, source_target_pairs={{18,34},{34,18},{50,66},{66,50},{82,98},{98,82},{114,130},{130,114... | collective-permute-start | bytes 61448 | tf_op jit(solution)/shard_map/ppermute | solution.py:422
  41.1 1.3 %collective-permute-start.8 = (f32[8,128]{1,0:T(8,128)S(1)}, f32[8,128]{1,0:T(8,128)S(1)}, u32[]{:S(2)}, u32[]{:S(2)}) collective-permute-start(f32[8,128]{1,0:T(8,128)S(1)} %get-tuple-element.55), channel_id=1, source_target_pairs={{498,1},{3,500},{502,5},{7,504},{506,9},{11,508},{510,13},{15,495}... | collective-permute-start | bytes 12296 | tf_op jit(solution)/shard_map/ppermute | solution.py:422
  42.4 0.0 copy-done
  42.4 2.4 %shard_map.94 = (f32[75,8,128]{2,1,0:T(8,128)S(1)}, f32[75,8,128]{2,1,0:T(8,128)S(1)}, f32[75,8,128]{2,1,0:T(8,128)S(1)}, f32[75,8,128]{2,1,0:T(8,128)S(1)}, f32...) custom-call(f32[600,128]{1,0:T(8,128)S(1)} %get-tuple-element.30.refs_0_, ...), custom_call_target="tpu_custom_call" | custom-call | tf_op jit(solution)/shard_map/pallas_call | solution.py:374
  44.9 11.7 %collective-permute-done.8.refs_20_ = f32[8,128]{1,0:T(8,128)S(1)} collective-permute-done((f32[8,128]{1,0:T(8,128)S(1)}, f32[8,128]{1,0:T(8,128)S(1)}, u32[]{:S(2)}, u32[]{:S(2)}) %collective-permute-start.8) | collective-permute-done | bytes 4128 | tf_op jit(solution)/shard_map/ppermute | solution.py:422
  56.5 0.0 collective-permute-done.2.refs_12_
  56.5 0.0 collective-permute-done.6.refs_18_
  56.5 0.0 collective-permute-done.7.refs_19_
  56.6 0.0 collective-permute-done.5.refs_13_
  56.6 2.4 %shard_map.99 = (f32[75,8,128]{2,1,0:T(8,128)}, f32[75,8,128]{2,1,0:T(8,128)}, f32[75,8,128]{2,1,0:T(8,128)}, f32[75,8,128]{2,1,0:T(8,128)}) custom-call(f32[75,8,128]{2,1,0:T(8,128)S(1)} %get-tuple-element.42.refs_0_, f32[75,8,128]{2,1,0:T(8,128)S(1)} %get-tuple-element.43.refs_1_, f32[75,8,128]{2,1,0:T(8,128)S(1)} %get-tuple-element.44.refs_2_, ...), custom_call_target="tpu_custom_call" | custom-call | tf_op jit(solution)/shard_map/pallas_call | solution.py:374
  (3 shorter events, 0.1 us)
Async XLA Ops:
  2.0 3.3 %collective-permute-start = (f32[304,128]{1,0:T(8,128)S(1)}, f32[304,128]{1,0:T(8,128)S(1)}, u32[]{:S(2)}, u32[]{:S(2)}) collective-permute-start(f32[304,128]{1,0:T(8,128)S(1)} %get-tuple-element.49.refs_8_), channel_id=1, source_target_pairs={{0,1},{1,0},{4,5},{5,4},{8,9},{9,8},{12,13},{13,12},{16,17},{17,16... | collective-permute-start | bytes 466952 | tf_op jit(solution)/shard_map/ppermute | solution.py:422
  4.0 35.8 %collective-permute-start.1 = (f32[304,128]{1,0:T(8,128)S(1)}, f32[304,128]{1,0:T(8,128)S(1)}, u32[]{:S(2)}, u32[]{:S(2)}) collective-permute-start(f32[304,128]{1,0:T(8,128)S(1)} %get-tuple-element.49.refs_8_), channel_id=1, source_target_pairs={{2,3},{3,2},{6,7},{7,6},{10,11},{11,10},{14,15},{15,14},{18,19},{1... | collective-permute-start | bytes 466952 | tf_op jit(solution)/shard_map/ppermute | solution.py:422
  6.0 19.6 %collective-permute-start.3 = (f32[40,128]{1,0:T(8,128)S(1)}, f32[40,128]{1,0:T(8,128)S(1)}, u32[]{:S(2)}, u32[]{:S(2)}) collective-permute-start(f32[40,128]{1,0:T(8,128)S(1)} %get-tuple-element.51.refs_6_), channel_id=1, source_target_pairs={{0,16},{16,0},{32,48},{48,32},{64,80},{80,64},{96,112},{112,96},{1... | collective-permute-start | bytes 61448 | tf_op jit(solution)/shard_map/ppermute | solution.py:422
  9.5 16.5 %collective-permute-start.4 = (f32[40,128]{1,0:T(8,128)S(1)}, f32[40,128]{1,0:T(8,128)S(1)}, u32[]{:S(2)}, u32[]{:S(2)}) collective-permute-start(f32[40,128]{1,0:T(8,128)S(1)} %get-tuple-element.52.refs_7_), channel_id=1, source_target_pairs={{16,32},{32,16},{48,64},{64,48},{80,96},{96,80},{112,128},{128,112... | collective-permute-start | bytes 61448 | tf_op jit(solution)/shard_map/ppermute | solution.py:422
  24.3 32.2 %collective-permute-start.2 = (f32[304,128]{1,0:T(8,128)S(1)}, f32[304,128]{1,0:T(8,128)S(1)}, u32[]{:S(2)}, u32[]{:S(2)}) collective-permute-start(f32[304,128]{1,0:T(8,128)S(1)} %get-tuple-element.50.refs_0_.refs_9_), channel_id=1, source_target_pairs={{2,1},{3,4},{6,5},{7,8},{10,9},{11,12},{14,13},{15,511},{18,17},{1... | collective-permute-start | bytes 466952 | tf_op jit(solution)/shard_map/ppermute | solution.py:422
  26.1 16.3 %copy-start = (f32[74,8,128]{2,1,0:T(8,128)S(1)}, f32[74,8,128]{2,1,0:T(8,128)}, u32[]{:S(2)}) copy-start(f32[74,8,128]{2,1,0:T(8,128)} %refs_4_.5) | copy-start | bytes 909316
  26.1 30.5 %collective-permute-start.5 = (f32[304,128]{1,0:T(8,128)S(1)}, f32[304,128]{1,0:T(8,128)S(1)}, u32[]{:S(2)}, u32[]{:S(2)}) collective-permute-start(f32[304,128]{1,0:T(8,128)S(1)} %shard_map.97), channel_id=1, source_target_pairs={{1,2},{4,3},{5,6},{8,7},{9,10},{12,11},{13,14},{17,18},{20,19},{21... | collective-permute-start | bytes 466952 | tf_op jit(solution)/shard_map/ppermute | solution.py:422
  39.8 16.8 %collective-permute-start.6 = (f32[40,128]{1,0:T(8,128)S(1)}, f32[40,128]{1,0:T(8,128)S(1)}, u32[]{:S(2)}, u32[]{:S(2)}) collective-permute-start(f32[40,128]{1,0:T(8,128)S(1)} %get-tuple-element.53.refs_14_), channel_id=1, source_target_pairs={{2,18},{18,2},{34,50},{50,34},{66,82},{82,66},{98,114},{114,98},{1... | collective-permute-start | bytes 61448 | tf_op jit(solution)/shard_map/ppermute | solution.py:422
  40.4 16.1 %collective-permute-start.7 = (f32[40,128]{1,0:T(8,128)S(1)}, f32[40,128]{1,0:T(8,128)S(1)}, u32[]{:S(2)}, u32[]{:S(2)}) collective-permute-start(f32[40,128]{1,0:T(8,128)S(1)} %get-tuple-element.54.refs_15_), channel_id=1, source_target_pairs={{18,34},{34,18},{50,66},{66,50},{82,98},{98,82},{114,130},{130,114... | collective-permute-start | bytes 61448 | tf_op jit(solution)/shard_map/ppermute | solution.py:422
  41.1 15.4 %collective-permute-start.8 = (f32[8,128]{1,0:T(8,128)S(1)}, f32[8,128]{1,0:T(8,128)S(1)}, u32[]{:S(2)}, u32[]{:S(2)}) collective-permute-start(f32[8,128]{1,0:T(8,128)S(1)} %get-tuple-element.55), channel_id=1, source_target_pairs={{498,1},{3,500},{502,5},{7,504},{506,9},{11,508},{510,13},{15,495}... | collective-permute-start | bytes 12296 | tf_op jit(solution)/shard_map/ppermute | solution.py:422

commit v5 on v3

--- a/solution.py
+++ b/solution.py
@@ -108,8 +108,8 @@
             west = jnp.zeros((ROWS, LANES), jnp.float32)
             for k in range(levels):
                 x = ref[k * ROWS : (k + 1) * ROWS, :]
-                east = jnp.where(lane == k, x[:, LANES - 1 : LANES], east)
-                west = jnp.where(lane == k, x[:, 0:1], west)
+                east = jnp.where(lane == k, roll(x, k + 1, 1), east)
+                west = jnp.where(lane == k, roll(x, k, 1), west)
             if f == 0:
                 east = jnp.where(lane == levels, h[:, LANES - 1 : LANES], east)
                 west = jnp.where(lane == levels, h[:, 0:1], west)
@@ -187,7 +187,8 @@
     lane, row = lane_ids(), row_ids()
     lat_even = lax.rem(lat, 2) == 0
     lon_even = lax.rem(lon, 2) == 0
-    b_first = jnp.logical_or(first, top)
+    k_first = jnp.logical_or(first, top)
+    b_first = jnp.logical_or(k_first, together(lon, mesh_size[1]))
     h = depth[...]
     f4 = (0.25 * DT) * coriolis_rows(lat, total)
     f7, f0 = f4[7:8, :], f4[0:1, :]
@@ -264,7 +265,7 @@
 
     (te, tw), (se, sw), (ue, uw), (ve, vw), (ce, cw) = (tiles(got_c, got_d, f) for f in range(5))
     (t9, tz), (s9, sz), (u9, uz), (v9, vz) = (tiles(own_c, own_d, f) for f in range(4))
-    cb = jnp.where(b_first, corner_p[...], corner_q[...])
+    cb = jnp.where(k_first, corner_p[...], corner_q[...])
     cb_u = jnp.broadcast_to(cb[0:1, :], (ROWS, LANES))
     cb_v = jnp.broadcast_to(cb[1:2, :], (ROWS, LANES))
     south_east = jnp.where(lat_even, cb_v, ce)
@@ -297,7 +298,6 @@
     at_n, at_s = row == ROWS - 1, row == 0
     at_e, at_w = lane == LANES - 1, lane == 0
     inner, last = elimination_constants(levels)
-    head = levels % UNROLL + UNROLL
     sides = ((dt_e, dt_w), (ds_e, ds_w), (du_e, du_w), (dv_e, dv_w))
 
     def down(k, c, carry):
@@ -311,7 +311,7 @@
                 n = n - extra
             base = jnp.where(at_n, n, jnp.where(at_s, south[f, one, :], 0.0))
             de = pltpu.roll(sides[f][0], LANES - 1 - k, 1)
-            dw = pltpu.roll(sides[f][1], lax.rem(LANES - k, LANES), 1)
+            dw = pltpu.roll(sides[f][1], (LANES - k) % LANES, 1)
             return base + jnp.where(at_e, de, jnp.where(at_w, dw, 0.0))
 
         dn = north[4, one, :]
@@ -342,13 +342,10 @@
 
     zero = h - h
     carry = (zero, zero, zero, zero, zero[0:1, :])
-    for k in range(head):
+    for k in range(levels):
         carry = down(k, k, carry)
-    carry = lax.fori_loop(head, levels, lambda k, x: down(k, head, x), carry, unroll=UNROLL)
-    carry = lax.fori_loop(
-        head, levels, lambda i, x: up(levels - 1 + head - i, head, x), (zero,) * 4, unroll=UNROLL
-    )
-    for k in range(head - 1, -1, -1):
+    carry = (zero,) * 4
+    for k in range(levels - 1, -1, -1):
         carry = up(k, k, carry)
 
 
@@ -373,6 +370,10 @@
     )(*far, *near)
 
 
+def together(lon, n_lon):
+    return (lon >= n_lon // 2) & (lon < n_lon * 7 // 8)
+
+
 def exchanges(n_lat, n_lon):
     def at(lat, lon):
         return (lon % n_lon) * n_lat + lat
@@ -386,7 +387,8 @@
             p["a_p" if lat % 4 < 2 else "a_q"] += both(at(lat, lon), at(lat + 1, lon))
         for lat in range(1, n_lat - 1, 2):
             for x, y in both((lat, lon), (lat + 1, lon)):
-                p["b_p" if y[0] % 4 < 2 else "b_q"].append((at(*x), at(*y)))
+                now = y[0] % 4 < 2 or together(lon, n_lon)
+                p["b_p" if now else "b_q"].append((at(*x), at(*y)))
             for x, y in both((lat, lon), (lat + 1, lon - 1)):
                 p["k_p" if y[0] % 4 < 2 else "k_q"].append((at(*x), at(*y)))
         p["b_p"].append((at(n_lat - 1, lon), at(n_lat - 1, n_lon - 1 - lon)))

time: 63 us -> 61.7 us (0.979)
  Pallas kernels: 8.25 us -> 7.02 us
    pallas_call x6, Pallas kernels: 8.25 us -> 7.02 us  [call(): pl.pallas_call(body, out_shape=shapes, in_specs=[HBM] * len(far) + [VMEM]...]
where the time goes in v5:
time: 61.7 us; the launch traced here: 61.4 us
  starting transfers between devices  53.6 us (87%)
  Pallas kernels  7.02 us (11%)
  between operations  0.84 us (1%)
    ppermute x10, starting transfers between devices, send(): return lax.ppermute(x, ('lon', 'lat'), pairs[name])  53.6 us
    pallas_call x6, Pallas kernels, call(): pl.pallas_call(body, out_shape=shapes, in_specs=[HBM] * len(far) + [VMEM]...  7.02 us
  transfers between devices with their start and end apart: 10, of which 0 were waited for; matrix products, arithmetic and copies ran while one was open for 0% of the time, Pallas kernels for 5%

profile of v5, /device:TPU:6, one launch (start us, length us, event | category | flops | bytes accessed | tf_op | source)
XLA Modules:
  0.0 61.4 jit_solution(16079815294870266422)
XLA Ops:
  0.6 1.4 %shard_map.93 = (f32[600,128]{1,0:T(8,128)S(1)}, f32[600,128]{1,0:T(8,128)S(1)}, f32[600,128]{1,0:T(8,128)S(1)}, f32[600,128]{1,0:T(8,128)S(1)}, f32[8,128]{1,0:...) custom-call(f32[600,128]{1,0:T(8,128)} %bitcast.4, f32[600,128]{1,0:T(8,128)} %bitcast.5, ...), custom_call_target="tpu_custom_call" | custom-call | tf_op jit(solution)/shard_map/pallas_call | solution.py:362
  2.0 1.9 %collective-permute-start = (f32[304,128]{1,0:T(8,128)S(1)}, f32[304,128]{1,0:T(8,128)S(1)}, u32[]{:S(2)}, u32[]{:S(2)}) collective-permute-start(f32[304,128]{1,0:T(8,128)S(1)} %get-tuple-element.49.refs_8_), channel_id=1, source_target_pairs={{0,1},{1,0},{4,5},{5,4},{8,9},{9,8},{12,13},{13,12},{16,17},{17,16... | collective-permute-start | bytes 466952 | tf_op jit(solution)/shard_map/ppermute | solution.py:414
  4.0 0.7 %collective-permute-start.1 = (f32[304,128]{1,0:T(8,128)S(1)}, f32[304,128]{1,0:T(8,128)S(1)}, u32[]{:S(2)}, u32[]{:S(2)}) collective-permute-start(f32[304,128]{1,0:T(8,128)S(1)} %get-tuple-element.49.refs_8_), channel_id=1, source_target_pairs={{2,3},{3,2},{6,7},{7,6},{10,11},{11,10},{14,15},{15,14},{18,19},{1... | collective-permute-start | bytes 466952 | tf_op jit(solution)/shard_map/ppermute | solution.py:414
  4.6 1.3 %collective-permute-start.2 = (f32[304,128]{1,0:T(8,128)S(1)}, f32[304,128]{1,0:T(8,128)S(1)}, u32[]{:S(2)}, u32[]{:S(2)}) collective-permute-start(f32[304,128]{1,0:T(8,128)S(1)} %get-tuple-element.50.refs_9_), channel_id=1, source_target_pairs={{2,1},{3,4},{6,5},{7,8},{10,9},{11,12},{14,13},{15,511},{18,17},{1... | collective-permute-start | bytes 466952 | tf_op jit(solution)/shard_map/ppermute | solution.py:414
  5.9 16.1 %collective-permute-start.3 = (f32[304,128]{1,0:T(8,128)S(1)}, f32[304,128]{1,0:T(8,128)S(1)}, u32[]{:S(2)}, u32[]{:S(2)}) collective-permute-start(f32[304,128]{1,0:T(8,128)S(1)} %get-tuple-element.50.refs_9_), channel_id=1, source_target_pairs={{1,2},{4,3},{5,6},{8,7},{9,10},{12,11},{13,14},{17,18},{20,19},{21... | collective-permute-start | bytes 466952 | tf_op jit(solution)/shard_map/ppermute | solution.py:414
  22.0 1.3 %collective-permute-start.8 = (f32[8,128]{1,0:T(8,128)S(1)}, f32[8,128]{1,0:T(8,128)S(1)}, u32[]{:S(2)}, u32[]{:S(2)}) collective-permute-start(f32[8,128]{1,0:T(8,128)S(1)} %get-tuple-element.55), channel_id=1, source_target_pairs={{498,1},{3,500},{502,5},{7,504},{506,9},{11,508},{510,13},{15,495}... | collective-permute-start | bytes 12296 | tf_op jit(solution)/shard_map/ppermute | solution.py:414
  23.3 0.0 collective-permute-done.refs_5_.refs_10_
  23.4 14.8 %collective-permute-start.9 = (f32[8,128]{1,0:T(8,128)S(1)}, f32[8,128]{1,0:T(8,128)S(1)}, u32[]{:S(2)}, u32[]{:S(2)}) collective-permute-start(f32[8,128]{1,0:T(8,128)S(1)} %get-tuple-element.55), channel_id=1, source_target_pairs={{1,498},{500,3},{5,502},{504,7},{9,506},{508,11},{13,510},{17,2},{... | collective-permute-start | bytes 12296 | tf_op jit(solution)/shard_map/ppermute | solution.py:414
  38.1 0.7 %shard_map.96 = (f32[40,128]{1,0:T(8,128)S(1)}, f32[40,128]{1,0:T(8,128)S(1)}) custom-call(f32[600,128]{1,0:T(8,128)S(1)} %get-tuple-element.30.refs_0_, f32[600,128]{1,0:T(8,128)S(1)} %get-tuple-element.31.refs_1_, f32[600,128]{1,0:T(8,128)S(1)} %get-tuple-element.32.refs_2_, f32[600,128]{1,0:T(8,128)S(1)} %get-tuple-element.33.refs_3_, ...), custom_call_target="tpu_custom_call" | custom-call | tf_op jit(solution)/shard_map/pallas_call | solution.py:362
  38.9 0.0 collective-permute-done.1.refs_5_.refs_11_
  38.9 3.5 %collective-permute-start.4 = (f32[40,128]{1,0:T(8,128)S(1)}, f32[40,128]{1,0:T(8,128)S(1)}, u32[]{:S(2)}, u32[]{:S(2)}) collective-permute-start(f32[40,128]{1,0:T(8,128)S(1)} %get-tuple-element.51.refs_6_), channel_id=1, source_target_pairs={{0,16},{16,0},{32,48},{48,32},{64,80},{80,64},{96,112},{112,96},{1... | collective-permute-start | bytes 61448 | tf_op jit(solution)/shard_map/ppermute | solution.py:414
  42.4 0.0 copy-start
  42.4 0.0 collective-permute-done.8.refs_20_
  42.5 12.7 %collective-permute-start.5 = (f32[40,128]{1,0:T(8,128)S(1)}, f32[40,128]{1,0:T(8,128)S(1)}, u32[]{:S(2)}, u32[]{:S(2)}) collective-permute-start(f32[40,128]{1,0:T(8,128)S(1)} %get-tuple-element.52.refs_7_), channel_id=1, source_target_pairs={{16,32},{32,16},{48,64},{64,48},{80,96},{96,80},{112,128},{128,112... | collective-permute-start | bytes 61448 | tf_op jit(solution)/shard_map/ppermute | solution.py:414
  55.2 0.0 collective-permute-done.9.refs_21_
  55.2 0.7 %collective-permute-start.6 = (f32[40,128]{1,0:T(8,128)S(1)}, f32[40,128]{1,0:T(8,128)S(1)}, u32[]{:S(2)}, u32[]{:S(2)}) collective-permute-start(f32[40,128]{1,0:T(8,128)S(1)} %get-tuple-element.53.refs_14_), channel_id=1, source_target_pairs={{2,18},{18,2},{34,50},{50,34},{66,82},{82,66},{98,114},{114,98},{1... | collective-permute-start | bytes 61448 | tf_op jit(solution)/shard_map/ppermute | solution.py:414
  55.8 0.0 collective-permute-done.2.refs_12_
  55.9 0.7 %collective-permute-start.7 = (f32[40,128]{1,0:T(8,128)S(1)}, f32[40,128]{1,0:T(8,128)S(1)}, u32[]{:S(2)}, u32[]{:S(2)}) collective-permute-start(f32[40,128]{1,0:T(8,128)S(1)} %get-tuple-element.54.refs_15_), channel_id=1, source_target_pairs={{18,34},{34,18},{50,66},{66,50},{82,98},{98,82},{114,130},{130,114... | collective-permute-start | bytes 61448 | tf_op jit(solution)/shard_map/ppermute | solution.py:414
  56.5 2.4 %shard_map.94 = (f32[75,8,128]{2,1,0:T(8,128)S(1)}, f32[75,8,128]{2,1,0:T(8,128)S(1)}, f32[75,8,128]{2,1,0:T(8,128)S(1)}, f32[75,8,128]{2,1,0:T(8,128)S(1)}, f32...) custom-call(f32[600,128]{1,0:T(8,128)S(1)} %get-tuple-element.30.refs_0_, ...), custom_call_target="tpu_custom_call" | custom-call | tf_op jit(solution)/shard_map/pallas_call | solution.py:362
  59.0 0.0 collective-permute-done.3.refs_13_
  59.0 0.0 collective-permute-done.4.refs_16_
  59.0 0.0 collective-permute-done.6.refs_18_
  59.0 0.0 collective-permute-done.7.refs_19_
  59.1 2.4 %shard_map.98 = (f32[75,8,128]{2,1,0:T(8,128)}, f32[75,8,128]{2,1,0:T(8,128)}, f32[75,8,128]{2,1,0:T(8,128)}, f32[75,8,128]{2,1,0:T(8,128)}) custom-call(f32[75,8,128]{2,1,0:T(8,128)S(1)} %get-tuple-element.42.refs_0_, f32[75,8,128]{2,1,0:T(8,128)S(1)} %get-tuple-element.43.refs_1_, f32[75,8,128]{2,1,0:T(8,128)S(1)} %get-tuple-element.44.refs_2_, ...), custom_call_target="tpu_custom_call" | custom-call | tf_op jit(solution)/shard_map/pallas_call | solution.py:362
  (4 shorter events, 0.1 us)
Async XLA Ops:
  2.0 21.3 %collective-permute-start = (f32[304,128]{1,0:T(8,128)S(1)}, f32[304,128]{1,0:T(8,128)S(1)}, u32[]{:S(2)}, u32[]{:S(2)}) collective-permute-start(f32[304,128]{1,0:T(8,128)S(1)} %get-tuple-element.49.refs_8_), channel_id=1, source_target_pairs={{0,1},{1,0},{4,5},{5,4},{8,9},{9,8},{12,13},{13,12},{16,17},{17,16... | collective-permute-start | bytes 466952 | tf_op jit(solution)/shard_map/ppermute | solution.py:414
  4.0 34.9 %collective-permute-start.1 = (f32[304,128]{1,0:T(8,128)S(1)}, f32[304,128]{1,0:T(8,128)S(1)}, u32[]{:S(2)}, u32[]{:S(2)}) collective-permute-start(f32[304,128]{1,0:T(8,128)S(1)} %get-tuple-element.49.refs_8_), channel_id=1, source_target_pairs={{2,3},{3,2},{6,7},{7,6},{10,11},{11,10},{14,15},{15,14},{18,19},{1... | collective-permute-start | bytes 466952 | tf_op jit(solution)/shard_map/ppermute | solution.py:414
  4.6 51.2 %collective-permute-start.2 = (f32[304,128]{1,0:T(8,128)S(1)}, f32[304,128]{1,0:T(8,128)S(1)}, u32[]{:S(2)}, u32[]{:S(2)}) collective-permute-start(f32[304,128]{1,0:T(8,128)S(1)} %get-tuple-element.50.refs_9_), channel_id=1, source_target_pairs={{2,1},{3,4},{6,5},{7,8},{10,9},{11,12},{14,13},{15,511},{18,17},{1... | collective-permute-start | bytes 466952 | tf_op jit(solution)/shard_map/ppermute | solution.py:414
  5.9 53.1 %collective-permute-start.3 = (f32[304,128]{1,0:T(8,128)S(1)}, f32[304,128]{1,0:T(8,128)S(1)}, u32[]{:S(2)}, u32[]{:S(2)}) collective-permute-start(f32[304,128]{1,0:T(8,128)S(1)} %get-tuple-element.50.refs_9_), channel_id=1, source_target_pairs={{1,2},{4,3},{5,6},{8,7},{9,10},{12,11},{13,14},{17,18},{20,19},{21... | collective-permute-start | bytes 466952 | tf_op jit(solution)/shard_map/ppermute | solution.py:414
  22.0 20.4 %collective-permute-start.8 = (f32[8,128]{1,0:T(8,128)S(1)}, f32[8,128]{1,0:T(8,128)S(1)}, u32[]{:S(2)}, u32[]{:S(2)}) collective-permute-start(f32[8,128]{1,0:T(8,128)S(1)} %get-tuple-element.55), channel_id=1, source_target_pairs={{498,1},{3,500},{502,5},{7,504},{506,9},{11,508},{510,13},{15,495}... | collective-permute-start | bytes 12296 | tf_op jit(solution)/shard_map/ppermute | solution.py:414
  23.4 31.8 %collective-permute-start.9 = (f32[8,128]{1,0:T(8,128)S(1)}, f32[8,128]{1,0:T(8,128)S(1)}, u32[]{:S(2)}, u32[]{:S(2)}) collective-permute-start(f32[8,128]{1,0:T(8,128)S(1)} %get-tuple-element.55), channel_id=1, source_target_pairs={{1,498},{500,3},{5,502},{504,7},{9,506},{508,11},{13,510},{17,2},{... | collective-permute-start | bytes 12296 | tf_op jit(solution)/shard_map/ppermute | solution.py:414
  38.9 20.1 %collective-permute-start.4 = (f32[40,128]{1,0:T(8,128)S(1)}, f32[40,128]{1,0:T(8,128)S(1)}, u32[]{:S(2)}, u32[]{:S(2)}) collective-permute-start(f32[40,128]{1,0:T(8,128)S(1)} %get-tuple-element.51.refs_6_), channel_id=1, source_target_pairs={{0,16},{16,0},{32,48},{48,32},{64,80},{80,64},{96,112},{112,96},{1... | collective-permute-start | bytes 61448 | tf_op jit(solution)/shard_map/ppermute | solution.py:414
  42.4 14.1 %copy-start = (f32[74,8,128]{2,1,0:T(8,128)S(1)}, f32[74,8,128]{2,1,0:T(8,128)}, u32[]{:S(2)}) copy-start(f32[74,8,128]{2,1,0:T(8,128)} %refs_4_.5) | copy-start | bytes 909316
  42.5 16.6 %collective-permute-start.5 = (f32[40,128]{1,0:T(8,128)S(1)}, f32[40,128]{1,0:T(8,128)S(1)}, u32[]{:S(2)}, u32[]{:S(2)}) collective-permute-start(f32[40,128]{1,0:T(8,128)S(1)} %get-tuple-element.52.refs_7_), channel_id=1, source_target_pairs={{16,32},{32,16},{48,64},{64,48},{80,96},{96,80},{112,128},{128,112... | collective-permute-start | bytes 61448 | tf_op jit(solution)/shard_map/ppermute | solution.py:414
  55.2 3.9 %collective-permute-start.6 = (f32[40,128]{1,0:T(8,128)S(1)}, f32[40,128]{1,0:T(8,128)S(1)}, u32[]{:S(2)}, u32[]{:S(2)}) collective-permute-start(f32[40,128]{1,0:T(8,128)S(1)} %get-tuple-element.53.refs_14_), channel_id=1, source_target_pairs={{2,18},{18,2},{34,50},{50,34},{66,82},{82,66},{98,114},{114,98},{1... | collective-permute-start | bytes 61448 | tf_op jit(solution)/shard_map/ppermute | solution.py:414
  55.9 3.2 %collective-permute-start.7 = (f32[40,128]{1,0:T(8,128)S(1)}, f32[40,128]{1,0:T(8,128)S(1)}, u32[]{:S(2)}, u32[]{:S(2)}) collective-permute-start(f32[40,128]{1,0:T(8,128)S(1)} %get-tuple-element.54.refs_15_), channel_id=1, source_target_pairs={{18,34},{34,18},{50,66},{66,50},{82,98},{98,82},{114,130},{130,114... | collective-permute-start | bytes 61448 | tf_op jit(solution)/shard_map/ppermute | solution.py:414

commit v6 on v5

--- a/solution.py
+++ b/solution.py
@@ -255,7 +255,7 @@
         return jnp.where(first, c_p[at, :], c_q[at, :])
 
     def got_d(at):
-        return jnp.where(first, d_p[at, :], d_q[at, :])
+        return d_p[at, :] + d_q[at, :]
 
     def own_c(at):
         return c_own[at, :]
@@ -371,7 +371,7 @@
 
 
 def together(lon, n_lon):
-    return (lon >= n_lon // 2) & (lon < n_lon * 7 // 8)
+    return (lon >= n_lon * 5 // 8) & (lon < n_lon * 7 // 8)
 
 
 def exchanges(n_lat, n_lon):
@@ -397,7 +397,8 @@
         side = "p" if lat % 4 < 2 else "q"
         for lon in range(0, n_lon, 2):
             p["c_" + side] += both(at(lat, lon), at(lat, lon + 1))
-            p["d_" + side] += both(at(lat, lon + 1), at(lat, lon + 2))
+            edge = together(lon + 1, n_lon) != together((lon + 2) % n_lon, n_lon)
+            p["d_q" if edge else "d_" + side] += both(at(lat, lon + 1), at(lat, lon + 2))
     return p
 
 

time: 61.7 us -> 61.7 us (level)
  no operation moved by 1% of the time
where the time goes in v6:
time: 61.7 us; the launch traced here: 61.5 us
  starting transfers between devices  53.6 us (87%)
  Pallas kernels  7.02 us (11%)
  between operations  0.84 us (1%)
    ppermute x10, starting transfers between devices, send(): return lax.ppermute(x, ('lon', 'lat'), pairs[name])  53.6 us
    pallas_call x6, Pallas kernels, call(): pl.pallas_call(body, out_shape=shapes, in_specs=[HBM] * len(far) + [VMEM]...  7.02 us
  transfers between devices with their start and end apart: 10, of which 0 were waited for; matrix products, arithmetic and copies ran while one was open for 0% of the time, Pallas kernels for 5%

profile of v6, /device:TPU:6, one launch (start us, length us, event | category | flops | bytes accessed | tf_op | source)
XLA Modules:
  0.0 61.5 jit_solution(8256269434542819383)
XLA Ops:
  0.6 1.4 %shard_map.93 = (f32[600,128]{1,0:T(8,128)S(1)}, f32[600,128]{1,0:T(8,128)S(1)}, f32[600,128]{1,0:T(8,128)S(1)}, f32[600,128]{1,0:T(8,128)S(1)}, f32[8,128]{1,0:...) custom-call(f32[600,128]{1,0:T(8,128)} %bitcast.4, f32[600,128]{1,0:T(8,128)} %bitcast.5, ...), custom_call_target="tpu_custom_call" | custom-call | tf_op jit(solution)/shard_map/pallas_call | solution.py:362
  2.0 1.9 %collective-permute-start = (f32[304,128]{1,0:T(8,128)S(1)}, f32[304,128]{1,0:T(8,128)S(1)}, u32[]{:S(2)}, u32[]{:S(2)}) collective-permute-start(f32[304,128]{1,0:T(8,128)S(1)} %get-tuple-element.49.refs_8_), channel_id=1, source_target_pairs={{0,1},{1,0},{4,5},{5,4},{8,9},{9,8},{12,13},{13,12},{16,17},{17,16... | collective-permute-start | bytes 466952 | tf_op jit(solution)/shard_map/ppermute | solution.py:415
  4.0 0.7 %collective-permute-start.1 = (f32[304,128]{1,0:T(8,128)S(1)}, f32[304,128]{1,0:T(8,128)S(1)}, u32[]{:S(2)}, u32[]{:S(2)}) collective-permute-start(f32[304,128]{1,0:T(8,128)S(1)} %get-tuple-element.49.refs_8_), channel_id=1, source_target_pairs={{2,3},{3,2},{6,7},{7,6},{10,11},{11,10},{14,15},{15,14},{18,19},{1... | collective-permute-start | bytes 466952 | tf_op jit(solution)/shard_map/ppermute | solution.py:415
  4.6 1.3 %collective-permute-start.2 = (f32[304,128]{1,0:T(8,128)S(1)}, f32[304,128]{1,0:T(8,128)S(1)}, u32[]{:S(2)}, u32[]{:S(2)}) collective-permute-start(f32[304,128]{1,0:T(8,128)S(1)} %get-tuple-element.50.refs_9_), channel_id=1, source_target_pairs={{2,1},{3,4},{6,5},{7,8},{10,9},{11,12},{14,13},{15,511},{18,17},{1... | collective-permute-start | bytes 466952 | tf_op jit(solution)/shard_map/ppermute | solution.py:415
  5.9 16.1 %collective-permute-start.3 = (f32[304,128]{1,0:T(8,128)S(1)}, f32[304,128]{1,0:T(8,128)S(1)}, u32[]{:S(2)}, u32[]{:S(2)}) collective-permute-start(f32[304,128]{1,0:T(8,128)S(1)} %get-tuple-element.50.refs_9_), channel_id=1, source_target_pairs={{1,2},{4,3},{5,6},{8,7},{9,10},{12,11},{13,14},{17,18},{20,19},{21... | collective-permute-start | bytes 466952 | tf_op jit(solution)/shard_map/ppermute | solution.py:415
  22.0 1.3 %collective-permute-start.8 = (f32[8,128]{1,0:T(8,128)S(1)}, f32[8,128]{1,0:T(8,128)S(1)}, u32[]{:S(2)}, u32[]{:S(2)}) collective-permute-start(f32[8,128]{1,0:T(8,128)S(1)} %get-tuple-element.55), channel_id=1, source_target_pairs={{498,1},{3,500},{502,5},{7,504},{506,9},{11,508},{510,13},{15,495}... | collective-permute-start | bytes 12296 | tf_op jit(solution)/shard_map/ppermute | solution.py:415
  23.3 0.0 collective-permute-done.refs_5_.refs_10_
  23.4 14.8 %collective-permute-start.9 = (f32[8,128]{1,0:T(8,128)S(1)}, f32[8,128]{1,0:T(8,128)S(1)}, u32[]{:S(2)}, u32[]{:S(2)}) collective-permute-start(f32[8,128]{1,0:T(8,128)S(1)} %get-tuple-element.55), channel_id=1, source_target_pairs={{1,498},{500,3},{5,502},{504,7},{9,506},{508,11},{13,510},{17,2},{... | collective-permute-start | bytes 12296 | tf_op jit(solution)/shard_map/ppermute | solution.py:415
  38.1 0.7 %shard_map.96 = (f32[40,128]{1,0:T(8,128)S(1)}, f32[40,128]{1,0:T(8,128)S(1)}) custom-call(f32[600,128]{1,0:T(8,128)S(1)} %get-tuple-element.30.refs_0_, f32[600,128]{1,0:T(8,128)S(1)} %get-tuple-element.31.refs_1_, f32[600,128]{1,0:T(8,128)S(1)} %get-tuple-element.32.refs_2_, f32[600,128]{1,0:T(8,128)S(1)} %get-tuple-element.33.refs_3_, ...), custom_call_target="tpu_custom_call" | custom-call | tf_op jit(solution)/shard_map/pallas_call | solution.py:362
  38.9 0.0 collective-permute-done.1.refs_5_.refs_11_
  38.9 3.5 %collective-permute-start.4 = (f32[40,128]{1,0:T(8,128)S(1)}, f32[40,128]{1,0:T(8,128)S(1)}, u32[]{:S(2)}, u32[]{:S(2)}) collective-permute-start(f32[40,128]{1,0:T(8,128)S(1)} %get-tuple-element.51.refs_6_), channel_id=1, source_target_pairs={{0,16},{16,0},{32,48},{48,32},{64,80},{80,64},{96,112},{112,96},{1... | collective-permute-start | bytes 61448 | tf_op jit(solution)/shard_map/ppermute | solution.py:415
  42.4 0.0 copy-start
  42.4 0.0 collective-permute-done.8.refs_20_
  42.5 12.7 %collective-permute-start.5 = (f32[40,128]{1,0:T(8,128)S(1)}, f32[40,128]{1,0:T(8,128)S(1)}, u32[]{:S(2)}, u32[]{:S(2)}) collective-permute-start(f32[40,128]{1,0:T(8,128)S(1)} %get-tuple-element.52.refs_7_), channel_id=1, source_target_pairs={{16,32},{32,16},{48,64},{64,48},{80,96},{96,80},{112,128},{128,112... | collective-permute-start | bytes 61448 | tf_op jit(solution)/shard_map/ppermute | solution.py:415
  55.2 0.0 collective-permute-done.9.refs_21_
  55.2 0.7 %collective-permute-start.6 = (f32[40,128]{1,0:T(8,128)S(1)}, f32[40,128]{1,0:T(8,128)S(1)}, u32[]{:S(2)}, u32[]{:S(2)}) collective-permute-start(f32[40,128]{1,0:T(8,128)S(1)} %get-tuple-element.53.refs_14_), channel_id=1, source_target_pairs={{2,18},{18,2},{34,50},{50,34},{66,82},{82,66},{98,114},{114,98},{1... | collective-permute-start | bytes 61448 | tf_op jit(solution)/shard_map/ppermute | solution.py:415
  55.8 0.0 collective-permute-done.2.refs_12_
  55.9 0.7 %collective-permute-start.7 = (f32[40,128]{1,0:T(8,128)S(1)}, f32[40,128]{1,0:T(8,128)S(1)}, u32[]{:S(2)}, u32[]{:S(2)}) collective-permute-start(f32[40,128]{1,0:T(8,128)S(1)} %get-tuple-element.54.refs_15_), channel_id=1, source_target_pairs={{304,320},{320,304},{432,448},{448,432},{305,321},{321,305},{433,4... | collective-permute-start | bytes 61448 | tf_op jit(solution)/shard_map/ppermute | solution.py:415
  56.5 2.4 %shard_map.94 = (f32[75,8,128]{2,1,0:T(8,128)S(1)}, f32[75,8,128]{2,1,0:T(8,128)S(1)}, f32[75,8,128]{2,1,0:T(8,128)S(1)}, f32[75,8,128]{2,1,0:T(8,128)S(1)}, f32...) custom-call(f32[600,128]{1,0:T(8,128)S(1)} %get-tuple-element.30.refs_0_, ...), custom_call_target="tpu_custom_call" | custom-call | tf_op jit(solution)/shard_map/pallas_call | solution.py:362
  59.0 0.0 collective-permute-done.3.refs_13_
  59.0 0.0 collective-permute-done.4.refs_16_
  59.0 0.0 collective-permute-done.6.refs_18_
  59.0 0.0 collective-permute-done.7.refs_19_
  59.1 2.4 %shard_map.98 = (f32[75,8,128]{2,1,0:T(8,128)}, f32[75,8,128]{2,1,0:T(8,128)}, f32[75,8,128]{2,1,0:T(8,128)}, f32[75,8,128]{2,1,0:T(8,128)}) custom-call(f32[75,8,128]{2,1,0:T(8,128)S(1)} %get-tuple-element.42.refs_0_, f32[75,8,128]{2,1,0:T(8,128)S(1)} %get-tuple-element.43.refs_1_, f32[75,8,128]{2,1,0:T(8,128)S(1)} %get-tuple-element.44.refs_2_, ...), custom_call_target="tpu_custom_call" | custom-call | tf_op jit(solution)/shard_map/pallas_call | solution.py:362
  (4 shorter events, 0.1 us)
Async XLA Ops:
  2.0 21.3 %collective-permute-start = (f32[304,128]{1,0:T(8,128)S(1)}, f32[304,128]{1,0:T(8,128)S(1)}, u32[]{:S(2)}, u32[]{:S(2)}) collective-permute-start(f32[304,128]{1,0:T(8,128)S(1)} %get-tuple-element.49.refs_8_), channel_id=1, source_target_pairs={{0,1},{1,0},{4,5},{5,4},{8,9},{9,8},{12,13},{13,12},{16,17},{17,16... | collective-permute-start | bytes 466952 | tf_op jit(solution)/shard_map/ppermute | solution.py:415
  4.0 34.9 %collective-permute-start.1 = (f32[304,128]{1,0:T(8,128)S(1)}, f32[304,128]{1,0:T(8,128)S(1)}, u32[]{:S(2)}, u32[]{:S(2)}) collective-permute-start(f32[304,128]{1,0:T(8,128)S(1)} %get-tuple-element.49.refs_8_), channel_id=1, source_target_pairs={{2,3},{3,2},{6,7},{7,6},{10,11},{11,10},{14,15},{15,14},{18,19},{1... | collective-permute-start | bytes 466952 | tf_op jit(solution)/shard_map/ppermute | solution.py:415
  4.6 51.2 %collective-permute-start.2 = (f32[304,128]{1,0:T(8,128)S(1)}, f32[304,128]{1,0:T(8,128)S(1)}, u32[]{:S(2)}, u32[]{:S(2)}) collective-permute-start(f32[304,128]{1,0:T(8,128)S(1)} %get-tuple-element.50.refs_9_), channel_id=1, source_target_pairs={{2,1},{3,4},{6,5},{7,8},{10,9},{11,12},{14,13},{15,511},{18,17},{1... | collective-permute-start | bytes 466952 | tf_op jit(solution)/shard_map/ppermute | solution.py:415
  5.9 53.1 %collective-permute-start.3 = (f32[304,128]{1,0:T(8,128)S(1)}, f32[304,128]{1,0:T(8,128)S(1)}, u32[]{:S(2)}, u32[]{:S(2)}) collective-permute-start(f32[304,128]{1,0:T(8,128)S(1)} %get-tuple-element.50.refs_9_), channel_id=1, source_target_pairs={{1,2},{4,3},{5,6},{8,7},{9,10},{12,11},{13,14},{17,18},{20,19},{21... | collective-permute-start | bytes 466952 | tf_op jit(solution)/shard_map/ppermute | solution.py:415
  22.0 20.4 %collective-permute-start.8 = (f32[8,128]{1,0:T(8,128)S(1)}, f32[8,128]{1,0:T(8,128)S(1)}, u32[]{:S(2)}, u32[]{:S(2)}) collective-permute-start(f32[8,128]{1,0:T(8,128)S(1)} %get-tuple-element.55), channel_id=1, source_target_pairs={{498,1},{3,500},{502,5},{7,504},{506,9},{11,508},{510,13},{15,495}... | collective-permute-start | bytes 12296 | tf_op jit(solution)/shard_map/ppermute | solution.py:415
  23.4 31.8 %collective-permute-start.9 = (f32[8,128]{1,0:T(8,128)S(1)}, f32[8,128]{1,0:T(8,128)S(1)}, u32[]{:S(2)}, u32[]{:S(2)}) collective-permute-start(f32[8,128]{1,0:T(8,128)S(1)} %get-tuple-element.55), channel_id=1, source_target_pairs={{1,498},{500,3},{5,502},{504,7},{9,506},{508,11},{13,510},{17,2},{... | collective-permute-start | bytes 12296 | tf_op jit(solution)/shard_map/ppermute | solution.py:415
  38.9 20.1 %collective-permute-start.4 = (f32[40,128]{1,0:T(8,128)S(1)}, f32[40,128]{1,0:T(8,128)S(1)}, u32[]{:S(2)}, u32[]{:S(2)}) collective-permute-start(f32[40,128]{1,0:T(8,128)S(1)} %get-tuple-element.51.refs_6_), channel_id=1, source_target_pairs={{0,16},{16,0},{32,48},{48,32},{64,80},{80,64},{96,112},{112,96},{1... | collective-permute-start | bytes 61448 | tf_op jit(solution)/shard_map/ppermute | solution.py:415
  42.4 14.1 %copy-start = (f32[74,8,128]{2,1,0:T(8,128)S(1)}, f32[74,8,128]{2,1,0:T(8,128)}, u32[]{:S(2)}) copy-start(f32[74,8,128]{2,1,0:T(8,128)} %refs_4_.5) | copy-start | bytes 909316
  42.5 16.6 %collective-permute-start.5 = (f32[40,128]{1,0:T(8,128)S(1)}, f32[40,128]{1,0:T(8,128)S(1)}, u32[]{:S(2)}, u32[]{:S(2)}) collective-permute-start(f32[40,128]{1,0:T(8,128)S(1)} %get-tuple-element.52.refs_7_), channel_id=1, source_target_pairs={{16,32},{32,16},{48,64},{64,48},{80,96},{96,80},{112,128},{128,112... | collective-permute-start | bytes 61448 | tf_op jit(solution)/shard_map/ppermute | solution.py:415
  55.2 3.9 %collective-permute-start.6 = (f32[40,128]{1,0:T(8,128)S(1)}, f32[40,128]{1,0:T(8,128)S(1)}, u32[]{:S(2)}, u32[]{:S(2)}) collective-permute-start(f32[40,128]{1,0:T(8,128)S(1)} %get-tuple-element.53.refs_14_), channel_id=1, source_target_pairs={{2,18},{18,2},{34,50},{50,34},{66,82},{82,66},{98,114},{114,98},{1... | collective-permute-start | bytes 61448 | tf_op jit(solution)/shard_map/ppermute | solution.py:415
  55.9 3.2 %collective-permute-start.7 = (f32[40,128]{1,0:T(8,128)S(1)}, f32[40,128]{1,0:T(8,128)S(1)}, u32[]{:S(2)}, u32[]{:S(2)}) collective-permute-start(f32[40,128]{1,0:T(8,128)S(1)} %get-tuple-element.54.refs_15_), channel_id=1, source_target_pairs={{304,320},{320,304},{432,448},{448,432},{305,321},{321,305},{433,4... | collective-permute-start | bytes 61448 | tf_op jit(solution)/shard_map/ppermute | solution.py:415
